TPU v7x, 32 devices: a whole 2x2x4 slice. The times are simulated.
32 devices in a mesh: seq: 8 (over y, x, core), doc: 4 (over z).
Axes of the slice: x: 2, y: 2, z: 4, core: 2. Of those that a mesh axis runs over, the one named last changes fastest.
Arguments:
- tokens: bfloat16 [4, 4096, 1024], P('doc', 'seq'), may hold values from -6 to 6
- cotangent: bfloat16 [4, 4096, 1024], P('doc', 'seq'), may hold values from -6 to 6
- attn_gain: bfloat16 [1024], replicated, may hold values from 0.5 to 1.5
- w_query: bfloat16 [1024, 1024], replicated, may hold values from -0.1875 to 0.1875
- w_key: bfloat16 [1024, 1024], replicated, may hold values from -0.1875 to 0.1875
- w_value: bfloat16 [1024, 1024], replicated, may hold values from -0.1875 to 0.1875
- w_out: bfloat16 [1024, 1024], replicated, may hold values from -3 to 3
- ffn_gain: bfloat16 [1024], replicated, may hold values from 0.5 to 1.5
- w_gate: bfloat16 [1024, 2816], replicated, may hold values from -0.1875 to 0.1875
- w_up: bfloat16 [1024, 2816], replicated, may hold values from -0.1875 to 0.1875
- w_down: bfloat16 [2816, 1024], replicated, may hold values from -0.109375 to 0.109375
- mem_keys: bfloat16 [4, 4096, 1024], P('doc', 'seq'), may hold values from -6 to 6
- mem_values: bfloat16 [4, 4096, 1024], P('doc', 'seq'), may hold values from -6 to 6
- seg_len: int32 [4, 2], P('doc'), may hold values from 512 to 2048, as said below
- mem_idx: int32 [4, 8, 128], P('doc', 'seq'), may hold values from 0 to 4095, as said below
Outputs:
- layer_out: bfloat16 [4, 4096, 1024], P('doc', 'seq')
- grad_tokens: bfloat16 [4, 4096, 1024], P('doc', 'seq')
- grad_attn_gain: float32 [1024], P(('seq', 'doc'))
- grad_query: float32 [1024, 1024], P(('seq', 'doc'))
- grad_key: float32 [1024, 1024], P(('seq', 'doc'))
- grad_value: float32 [1024, 1024], P(('seq', 'doc'))
- grad_out: float32 [1024, 1024], P(('seq', 'doc'))
- grad_ffn_gain: float32 [1024], P(('seq', 'doc'))
- grad_gate: float32 [1024, 2816], P(('seq', 'doc'))
- grad_up: float32 [1024, 2816], P(('seq', 'doc'))
- grad_down: float32 [2816, 1024], P(('seq', 'doc'))
- grad_mem_keys: float32 [4, 4096, 1024], P('doc', 'seq')
- grad_mem_values: float32 [4, 4096, 1024], P('doc', 'seq')
Inputs may be any that keep to these rules, and one draw needn't show every extreme that they name: Positions at or beyond seg_len in a segment are padding; in every stream some segment has all 2048 positions valid. `mem_idx`: memory row r of a stream lies on seq index r // 512. Each query block names exactly 32 distinct rows of each of half of the seq indices and none of the others; which indices is drawn afresh for every block.
All inputs are finite; a program needn't handle non-finite values.
Results may differ from a plain program's by a relative error of at most 0.014.
Values may be sent and summed in bfloat16 or wider, within the bound.
A program may use at most 320 MiB of HBM per device.

v0:
```python
import functools
import math

import jax
import jax.numpy as jnp
from jax import lax
from jax.experimental import pallas as pl
from jax.experimental.pallas import tpu as pltpu
from jax.sharding import PartitionSpec as P

HEADS = 8
HEAD_DIM = 128
TOPK = 128
BPS = 4
NEG = -1000000000.0
MESH = pl.DeviceIdType.MESH
EPS = 1e-05
UNIT = 256
SKEW = 4


def flip(value, bit):
    return value + bit - 2 * bit * ((value // bit) % 2)


HALF = HEADS // 2
LOG2E = math.log2(math.e)
SCALE = HEAD_DIM ** (-0.5)
NT = (((1,), (1,)), ((), ()))
TN = (((0,), (0,)), ((), ()))
NN = (((1,), (0,)), ((), ()))


def matmul(left, right, dims):
    return lax.dot_general(left, right, dims, preferred_element_type=jnp.float32)


def seats():
    seq, doc = lax.axis_index("seq"), lax.axis_index("doc")
    core, chip = seq % 2, (seq // 2) % 2
    mate = (flip(seq, 1), doc)
    across = (flip(seq, 2), doc)
    diagonal = (flip(flip(seq, 2), 1), doc)
    return core, chip, mate, across, diagonal


def meet(peers):
    barrier = pltpu.get_barrier_semaphore()
    for peer in peers:
        pl.semaphore_signal(barrier, inc=1, device_id=peer, device_id_type=MESH)
    pl.semaphore_wait(barrier, len(peers))


def head_lanes(core, head):
    return pl.ds(pl.multiple_of((core * HALF + head) * HEAD_DIM, HEAD_DIM), HEAD_DIM)


def remote(src, dst, send, recv, peer):
    return pltpu.make_async_remote_copy(
        src_ref=src, dst_ref=dst, send_sem=send, recv_sem=recv, device_id=peer, device_id_type=MESH
    )


def share_heads(sources, boxes, core, mate, local_sem, send_sem, recv_sem):
    copies = []
    for i, (source, box) in enumerate(zip(sources, boxes)):
        for head in range(HALF):
            copies.append(
                remote(
                    source.at[:, head_lanes(1 - core, head)],
                    box.at[core, head],
                    send_sem.at[i, head],
                    recv_sem.at[i, head],
                    mate,
                )
            )
            copies[-1].start()
    for i, (source, box) in enumerate(zip(sources, boxes)):
        for head in range(HALF):
            copies.append(
                pltpu.make_async_copy(
                    source.at[:, head_lanes(core, head)], box.at[core, head], local_sem.at[i, head]
                )
            )
            copies[-1].start()
    return copies


def masked(scores, first_key, limit, diagonal):
    key = lax.broadcasted_iota(jnp.int32, scores.shape, 0)
    ok = key + first_key < limit
    if diagonal:
        ok = ok & (key <= lax.broadcasted_iota(jnp.int32, scores.shape, 1))
    return jnp.where(ok, scores, NEG)


def soften(parts):
    top = functools.reduce(
        jnp.maximum, [jnp.max(scores, axis=0, keepdims=True) for scores, _ in parts]
    )
    total, mixed = 0.0, 0.0
    for scores, values in parts:
        exponent = jnp.exp2(scores - top)
        total = total + jnp.sum(exponent, axis=0, keepdims=True)
        mixed = mixed + matmul(values, exponent.astype(jnp.bfloat16), TN)
    return mixed / total, top + jnp.log(total) * LOG2E


def forward_kernel(
    limit_ref, q, k, v, mk, mv,
    attended, qb, kb, vb, qx, mkb, mvb, ob, lse,
    mixed_own, mixed_out, mixed_in, lse_out, lse_in,
    local_sem, mate_send, mate_recv, far_send, far_recv, back_send, back_recv, end_sem,
):
    core, chip, mate, across, diagonal = seats()
    block = q.shape[0]
    limit = limit_ref[0]
    meet((mate, across, diagonal))

    def query_copy(head, own):
        return remote(
            q.at[:, head_lanes(core if own else 1 - core, head)],
            qx.at[core, head],
            far_send.at[0 if own else 1, head],
            far_recv.at[core, head],
            across if own else diagonal,
        )

    def arrived_query(far, head):
        return remote(
            q.at[:, head_lanes(core, head)], qx.at[far, head], far_send.at[0, head], far_recv.at[far, head], across
        )

    @pl.when(chip == 1)
    def _():
        for head in range(HALF):
            query_copy(head, True).start()
            query_copy(head, False).start()

    copies = share_heads((q, k, v, mk, mv), (qb, kb, vb, mkb, mvb), core, mate, local_sem, mate_send, mate_recv)
    for copy in copies:
        copy.wait()

    def own_part(blk, head):
        query = qb[blk, head]
        parts = []
        for kblk in range(blk + 1):
            scores = matmul(kb[kblk, head], query, NT) * (SCALE * LOG2E)
            scores = masked(scores, (2 * chip + kblk) * block, limit, kblk == blk)
            parts.append((scores, vb[kblk, head]))
        parts.append((matmul(mkb[blk, head], query, NT) * (SCALE * LOG2E), mvb[blk, head]))
        return soften(parts)

    for blk in range(2):
        def own_head(head, carry):
            mixed, level = own_part(blk, head)
            mixed_own[blk, head] = mixed
            lse[blk, head] = level
            return carry
        lax.fori_loop(0, HALF, own_head, 0)

    def back_copy(blk, head):
        return (
            remote(mixed_out.at[blk, head], mixed_in.at[blk, head], back_send.at[0, blk, head], back_recv.at[0, blk, head], across),
            remote(lse_out.at[blk, head], lse_in.at[blk, head], back_send.at[1, blk, head], back_recv.at[1, blk, head], across),
        )

    @pl.when(chip == 0)
    def _():
        def cross(i, carry):
            head, blk = i // 2, i % 2
            arrived_query(blk, head).wait_recv()
            query = qx[blk, head]
            parts = []
            for kblk in range(2):
                scores = matmul(kb[kblk, head], query, NT) * (SCALE * LOG2E)
                parts.append((masked(scores, kblk * block, limit, False), vb[kblk, head]))
            mixed, level = soften(parts)
            mixed_out[blk, head] = mixed.astype(jnp.bfloat16)
            lse_out[blk, head] = level
            for copy in back_copy(blk, head):
                copy.start()
            return carry
        lax.fori_loop(0, 2 * HALF, cross, 0)

        def finish(i, carry):
            head, blk = i // 2, i % 2
            ob[blk, head] = mixed_own[blk, head].T.astype(jnp.bfloat16)
            return carry
        lax.fori_loop(0, 2 * HALF, finish, 0)

    @pl.when(chip == 1)
    def _():
        def merge(i, carry):
            head, blk = i // 2, i % 2
            for copy in back_copy(blk, head):
                copy.wait_recv()
            near, far = lse[blk, head], lse_in[blk, head]
            top = jnp.maximum(near, far)
            near, far = jnp.exp2(near - top), jnp.exp2(far - top)
            total = near + far
            mixed = (mixed_own[blk, head] * near + mixed_in[blk, head].astype(jnp.float32) * far) / total
            ob[blk, head] = mixed.T.astype(jnp.bfloat16)
            lse[blk, head] = top + jnp.log(total) * LOG2E
            return carry
        lax.fori_loop(0, 2 * HALF, merge, 0)

    ends = []
    for head in range(HALF):
        ends.append(
            remote(ob.at[1 - core, head], attended.at[:, head_lanes(core, head)], end_sem.at[0, head], end_sem.at[1, head], mate)
        )
        ends.append(
            pltpu.make_async_copy(ob.at[core, head], attended.at[:, head_lanes(core, head)], end_sem.at[2, head])
        )
    for copy in ends:
        copy.start()
    for copy in ends:
        copy.wait()

    @pl.when(chip == 0)
    def _():
        for head in range(HALF):
            for blk in range(2):
                for copy in back_copy(blk, head):
                    copy.wait_send()

    @pl.when(chip == 1)
    def _():
        for head in range(HALF):
            query_copy(head, True).wait_send()
            query_copy(head, False).wait_send()


def attend_forward(limit, queries, keys, values, mem_keys, mem_values):
    block, width = queries.shape
    topk = mem_keys.shape[0]
    low, full = jnp.bfloat16, jnp.float32
    box = (2, HALF, block, HEAD_DIM)
    mem_box = (2, HALF, topk, HEAD_DIM)
    flat = (2, HALF, HEAD_DIM, block)
    row = (2, HALF, 1, block)
    dma = pltpu.SemaphoreType.DMA
    hbm, vmem = pl.BlockSpec(memory_space=pl.ANY), pl.BlockSpec(memory_space=pltpu.VMEM)
    struct = jax.ShapeDtypeStruct
    return pl.pallas_call(
        forward_kernel,
        out_shape=(
            struct((block, width), low),
            struct(box, low), struct(box, low), struct(box, low), struct(box, low),
            struct(mem_box, low), struct(mem_box, low), struct(box, low), struct(row, full),
        ),
        in_specs=[pl.BlockSpec(memory_space=pltpu.SMEM)] + [hbm] * 5,
        out_specs=(hbm,) + (vmem,) * 8,
        scratch_shapes=[
            pltpu.VMEM(flat, full), pltpu.VMEM(flat, low), pltpu.VMEM(flat, low),
            pltpu.VMEM(row, full), pltpu.VMEM(row, full),
            dma((5, HALF)), dma((5, HALF)), dma((5, HALF)),
            dma((2, HALF)), dma((2, HALF)), dma((2, 2, HALF)), dma((2, 2, HALF)), dma((3, HALF)),
        ],
        name="attend_forward",
        compiler_params=pltpu.CompilerParams(collective_id=1, has_side_effects=True, vmem_limit_bytes=56 * 2**20),
    )(limit, queries, keys, values, mem_keys, mem_values)


def backward_kernel(
    limit_ref, grad, qb, kb, vb, qx, mkb, mvb, ob, lse,
    dq, dk, dv, dmk, dmv,
    gb, gx, delta, lse_in, delta_in, dq_own, dq_out, dq_in, dk_sum, dv_sum, dmk_low, dmv_low, dqb, dkb, dvb,
    local_sem, mate_send, mate_recv, far_send, far_recv, row_send, row_recv, back_send, back_recv,
    end_local, end_send, end_recv,
):
    core, chip, mate, across, diagonal = seats()
    block = grad.shape[0]
    limit = limit_ref[0]
    meet((mate, across, diagonal))

    def grad_copy(head, own):
        return remote(
            grad.at[:, head_lanes(core if own else 1 - core, head)],
            gx.at[core, head],
            far_send.at[0 if own else 1, head],
            far_recv.at[core, head],
            across if own else diagonal,
        )

    def arrived_grad(far, head):
        return remote(
            grad.at[:, head_lanes(core, head)], gx.at[far, head], far_send.at[0, head], far_recv.at[far, head], across
        )

    def row_copies():
        return (
            remote(lse, lse_in, row_send.at[0], row_recv.at[0], across),
            remote(delta, delta_in, row_send.at[1], row_recv.at[1], across),
        )

    @pl.when(chip == 1)
    def _():
        for head in range(HALF):
            grad_copy(head, True).start()
            grad_copy(head, False).start()

    copies = share_heads((grad,), (gb,), core, mate, local_sem, mate_send, mate_recv)
    for copy in copies:
        copy.wait()

    def rows(i, carry):
        head, blk = i // 2, i % 2
        product = gb[blk, head].astype(jnp.float32) * ob[blk, head].astype(jnp.float32)
        delta[blk, head] = jnp.sum(product.T, axis=0, keepdims=True)
        return carry

    lax.fori_loop(0, 2 * HALF, rows, 0)

    @pl.when(chip == 1)
    def _():
        for copy in row_copies():
            copy.start()

    def pull(key_rows, value_rows, query, grad_rows, level, inner, where):
        scores = matmul(key_rows, query, NT) * (SCALE * LOG2E)
        if where is not None:
            scores = masked(scores, where[0], limit, where[1])
        weights = jnp.exp2(scores - level)
        grad_weights = matmul(value_rows, grad_rows, NT)
        grad_scores = (weights * (grad_weights - inner)).astype(jnp.bfloat16)
        return (
            matmul(grad_scores, query, NN),
            matmul(weights.astype(jnp.bfloat16), grad_rows, NN),
            matmul(key_rows, grad_scores, TN),
        )

    for blk in range(2):
        def own_head(head, carry):
            query, grad_rows = qb[blk, head], gb[blk, head]
            level, inner = lse[blk, head], delta[blk, head]
            total = 0.0
            for kblk in range(blk + 1):
                gk, gv, gq = pull(
                    kb[kblk, head], vb[kblk, head], query, grad_rows, level, inner,
                    ((2 * chip + kblk) * block, kblk == blk),
                )
                if kblk == blk:
                    dk_sum[kblk, head], dv_sum[kblk, head] = gk, gv
                else:
                    dk_sum[kblk, head] += gk
                    dv_sum[kblk, head] += gv
                total = total + gq
            gk, gv, gq = pull(mkb[blk, head], mvb[blk, head], query, grad_rows, level, inner, None)
            dmk_low[blk, head] = (gk * SCALE).astype(jnp.bfloat16)
            dmv_low[blk, head] = gv.astype(jnp.bfloat16)
            dq_own[blk, head] = total + gq
            return carry
        lax.fori_loop(0, HALF, own_head, 0)

    def back_copy(blk, head):
        return remote(dq_out.at[blk, head], dq_in.at[blk, head], back_send.at[blk, head], back_recv.at[blk, head], across)

    @pl.when(chip == 0)
    def _():
        for copy in row_copies():
            copy.wait_recv()

        def cross(i, carry):
            head, blk = i // 2, i % 2
            arrived_grad(blk, head).wait_recv()
            query, grad_rows = qx[blk, head], gx[blk, head]
            level, inner = lse_in[blk, head], delta_in[blk, head]
            total = 0.0
            for kblk in range(2):
                gk, gv, gq = pull(
                    kb[kblk, head], vb[kblk, head], query, grad_rows, level, inner, (kblk * block, False)
                )
                dk_sum[kblk, head] += gk
                dv_sum[kblk, head] += gv
                total = total + gq
            dq_out[blk, head] = total.astype(jnp.bfloat16)
            back_copy(blk, head).start()
            return carry
        lax.fori_loop(0, 2 * HALF, cross, 0)

    def finish(i, carry):
        head, blk = i // 2, i % 2
        dqb[blk, head] = (dq_own[blk, head].T * SCALE).astype(jnp.bfloat16)
        dkb[blk, head] = (dk_sum[blk, head] * SCALE).astype(jnp.bfloat16)
        dvb[blk, head] = dv_sum[blk, head].astype(jnp.bfloat16)
        return carry

    @pl.when(chip == 1)
    def _():
        def merge(i, carry):
            head, blk = i // 2, i % 2
            back_copy(blk, head).wait_recv()
            dq_own[blk, head] += dq_in[blk, head].astype(jnp.float32)
            return finish(i, carry)
        lax.fori_loop(0, 2 * HALF, merge, 0)

    @pl.when(chip == 0)
    def _():
        lax.fori_loop(0, 2 * HALF, finish, 0)

    ends = []
    for i, (box, out) in enumerate(((dqb, dq), (dkb, dk), (dvb, dv), (dmk_low, dmk), (dmv_low, dmv))):
        for head in range(HALF):
            lanes = head_lanes(core, head)
            ends.append(remote(box.at[1 - core, head], out.at[:, lanes], end_send.at[i, head], end_recv.at[i, head], mate))
            ends.append(pltpu.make_async_copy(box.at[core, head], out.at[:, lanes], end_local.at[i, head]))
    for copy in ends:
        copy.start()
    for copy in ends:
        copy.wait()

    @pl.when(chip == 0)
    def _():
        for head in range(HALF):
            for blk in range(2):
                back_copy(blk, head).wait_send()

    @pl.when(chip == 1)
    def _():
        for copy in row_copies():
            copy.wait_send()
        for head in range(HALF):
            grad_copy(head, True).wait_send()
            grad_copy(head, False).wait_send()


def attend_backward(limit, grad, saved):
    block, width = grad.shape
    topk = saved[4].shape[2]
    low, full = jnp.bfloat16, jnp.float32
    box = (2, HALF, block, HEAD_DIM)
    mem_box = (2, HALF, topk, HEAD_DIM)
    flat = (2, HALF, HEAD_DIM, block)
    row = (2, HALF, 1, block)
    dma = pltpu.SemaphoreType.DMA
    hbm, vmem = pl.BlockSpec(memory_space=pl.ANY), pl.BlockSpec(memory_space=pltpu.VMEM)
    struct = jax.ShapeDtypeStruct
    return pl.pallas_call(
        backward_kernel,
        out_shape=(struct((block, width), low),) * 3 + (struct((topk, width), low),) * 2,
        in_specs=[pl.BlockSpec(memory_space=pltpu.SMEM), hbm] + [vmem] * 8,
        out_specs=(hbm,) * 5,
        scratch_shapes=[
            pltpu.VMEM(box, low), pltpu.VMEM(box, low),
            pltpu.VMEM(row, full), pltpu.VMEM(row, full), pltpu.VMEM(row, full),
            pltpu.VMEM(flat, full), pltpu.VMEM(flat, low), pltpu.VMEM(flat, low),
            pltpu.VMEM(box, full), pltpu.VMEM(box, full),
            pltpu.VMEM(mem_box, low), pltpu.VMEM(mem_box, low),
            pltpu.VMEM(box, low), pltpu.VMEM(box, low), pltpu.VMEM(box, low),
            dma((1, HALF)), dma((1, HALF)), dma((1, HALF)),
            dma((2, HALF)), dma((2, HALF)), dma((2,)), dma((2,)),
            dma((2, HALF)), dma((2, HALF)),
            dma((5, HALF)), dma((5, HALF)), dma((5, HALF)),
        ],
        name="attend_backward",
        compiler_params=pltpu.CompilerParams(collective_id=2, has_side_effects=True, vmem_limit_bytes=56 * 2**20),
    )(limit, grad, *saved)


def keep_order(rank_of):
    before = lax.broadcasted_iota(jnp.int32, (rank_of, rank_of), 0)
    return (before < lax.broadcasted_iota(jnp.int32, (rank_of, rank_of), 1)).astype(jnp.bfloat16)


def front_kernel(
    limit_ref, tokens, gain, w_query, w_key, w_value, mem_keys, mem_values, wanted,
    attended, qb, kb, vb, qx, mkb, mvb, ob, lse, spots, pick_t,
    rows, weights, normed, qkv, tables, every, pick, mem_out, mem_in,
    mixed_own, mixed_out, mixed_in, lse_out, lse_in,
    load_sem, want_send, want_recv, mem_send, mem_recv, mem_local,
    local_sem, mate_send, mate_recv, far_send, far_recv, back_send, back_recv, end_sem,
):
    core, chip, mate, across, diagonal = seats()
    seq, doc = lax.axis_index("seq"), lax.axis_index("doc")
    seq_count, capacity = mem_in.shape[0], mem_in.shape[3]
    block, width = tokens.shape
    mem_rows, topk = tables.shape[1], every.shape[2]
    limit = limit_ref[0]

    loads = [
        pltpu.make_async_copy(src, dst, load_sem.at[i])
        for i, (src, dst) in enumerate(
            (
                (wanted, every.at[seq]), (tokens, rows), (w_query, weights.at[0]), (w_key, weights.at[1]),
                (w_value, weights.at[2]), (mem_keys, tables.at[0]), (mem_values, tables.at[1]),
            )
        )
    ]
    for copy in loads:
        copy.start()
    meet([(lax.rem(seq + away, seq_count), doc) for away in range(1, seq_count)])
    loads[0].wait()

    def want_copy(away):
        return remote(
            every.at[seq], every.at[seq], want_send.at[away - 1], want_recv.at[away - 1],
            (lax.rem(seq + away, seq_count), doc),
        )

    def want_arrival(away):
        source = lax.rem(seq + seq_count - away, seq_count)
        return remote(every.at[source], every.at[source], want_send.at[away - 1], want_recv.at[away - 1], (source, doc))

    def mem_copy(away):
        peer = lax.rem(seq + away, seq_count)
        return remote(mem_out.at[peer], mem_in.at[seq], mem_send.at[away - 1], mem_recv.at[away - 1], (peer, doc))

    def mem_arrival(away):
        source = lax.rem(seq + seq_count - away, seq_count)
        return remote(mem_out.at[source], mem_in.at[source], mem_send.at[away - 1], mem_recv.at[away - 1], (source, doc))

    for away in range(1, seq_count):
        want_copy(away).start()
    loads[1].wait()
    part = 64

    def norm(i, carry):
        at = pl.ds(pl.multiple_of(i * part, part), part)
        x = rows[at, :].astype(jnp.float32)
        factor = lax.rsqrt(jnp.mean(x * x, axis=-1, keepdims=True) + EPS)
        normed[at, :] = (x * factor * gain[...]).astype(jnp.bfloat16)
        return carry

    lax.fori_loop(0, block // part, norm, 0)

    def project(i):
        loads[2 + i].wait()

        def one(j, carry):
            lanes = pl.ds(pl.multiple_of(j * UNIT, UNIT), UNIT)
            qkv[i, :, lanes] = matmul(normed[...], weights[i, :, lanes], NN).astype(jnp.bfloat16)
            return carry

        lax.fori_loop(0, width // UNIT, one, 0)

    project(0)

    def query_copy(head, own):
        return remote(
            qkv.at[0, :, head_lanes(core if own else 1 - core, head)],
            qx.at[core, head],
            far_send.at[0 if own else 1, head],
            far_recv.at[core, head],
            across if own else diagonal,
        )

    def arrived_query(far, head):
        return remote(
            qkv.at[0, :, head_lanes(core, head)], qx.at[far, head], far_send.at[0, head], far_recv.at[far, head], across
        )

    @pl.when(chip == 1)
    def _():
        for head in range(HALF):
            query_copy(head, True).start()
            query_copy(head, False).start()

    project(1)
    project(2)
    copies = share_heads(
        (qkv.at[0], qkv.at[1], qkv.at[2]), (qb, kb, vb), core, mate, local_sem, mate_send, mate_recv
    )

    for away in range(1, seq_count):
        want_arrival(away).wait_recv()
    triangle = keep_order(topk)
    asked = every[:, 0, :]
    here = asked - seq * mem_rows
    mine = (here >= 0) & (here < mem_rows)
    before = matmul(mine.astype(jnp.bfloat16), triangle, NN).astype(jnp.int32)
    place = lax.broadcasted_iota(jnp.int32, (capacity, topk), 0)
    line = lax.broadcasted_iota(jnp.int32, (mem_rows, topk), 0)
    for b in range(seq_count):
        at_place = jnp.where((before[b : b + 1] == place) & (here[b : b + 1] >= 0) & (here[b : b + 1] < mem_rows), 1.0, 0.0)
        at_line = jnp.where(here[b : b + 1] == line, 1.0, 0.0)
        pick[b * capacity : (b + 1) * capacity, :] = matmul(
            at_place.astype(jnp.bfloat16), at_line.astype(jnp.bfloat16), NT
        ).astype(jnp.bfloat16)
    half = HALF * HEAD_DIM
    for kind in range(2):
        loads[5 + kind].wait()
        for side in range(2):
            found = matmul(pick[...], tables[kind, :, side * half : (side + 1) * half], NN).astype(jnp.bfloat16)
            for b in range(seq_count):
                mem_out[2 * (b // 2) + side, b % 2, kind] = found[b * capacity : (b + 1) * capacity]
    for away in range(1, seq_count):
        mem_copy(away).start()
    own_rows = pltpu.make_async_copy(mem_out.at[seq], mem_in.at[seq], mem_local.at[0])
    own_rows.start()
    pick_t[...] = pick[...].astype(jnp.float32).T.astype(jnp.bfloat16)
    seat = lax.broadcasted_iota(jnp.int32, (seq_count, topk), 0)
    slot_at = lax.broadcasted_iota(jnp.int32, (seq_count * capacity, topk), 0)
    for blk in range(2):
        away_rows = every[2 * (seq // 2) + blk] - seat * mem_rows
        owner = (away_rows >= 0) & (away_rows < mem_rows)
        rank = matmul(owner.astype(jnp.bfloat16), triangle, NN).astype(jnp.int32)
        slot = jnp.sum(jnp.where(owner, seat * capacity + rank, 0), axis=0, keepdims=True)
        spots[blk] = jnp.where(slot == slot_at, 1.0, 0.0).astype(jnp.bfloat16)

    for copy in copies:
        copy.wait()

    def own_head(blk, head):
        query = qb[blk, head]
        parts = []
        for kblk in range(blk + 1):
            scores = matmul(kb[kblk, head], query, NT) * (SCALE * LOG2E)
            scores = masked(scores, (2 * chip + kblk) * block, limit, kblk == blk)
            parts.append((scores, vb[kblk, head]))
        mixed_own[blk, head], lse[blk, head] = soften(parts)

    def back_copy(blk, head):
        return (
            remote(mixed_out.at[blk, head], mixed_in.at[blk, head], back_send.at[0, blk, head], back_recv.at[0, blk, head], across),
            remote(lse_out.at[blk, head], lse_in.at[blk, head], back_send.at[1, blk, head], back_recv.at[1, blk, head], across),
        )

    def heads(head, carry):
        @pl.when(chip == 0)
        def _():
            def cross(blk, carry):
                arrived_query(blk, head).wait_recv()
                query = qx[blk, head]
                parts = []
                for kblk in range(2):
                    scores = matmul(kb[kblk, head], query, NT) * (SCALE * LOG2E)
                    parts.append((masked(scores, kblk * block, limit, False), vb[kblk, head]))
                mixed, level = soften(parts)
                mixed_out[blk, head] = mixed.astype(jnp.bfloat16)
                lse_out[blk, head] = level
                for copy in back_copy(blk, head):
                    copy.start()
                return carry

            lax.fori_loop(0, 2, cross, 0)

        own_head(0, head)
        own_head(1, head)
        return carry

    lax.fori_loop(0, HALF, heads, 0)

    for away in range(1, seq_count):
        mem_arrival(away).wait_recv()
    own_rows.wait()
    for blk in range(2):
        for kind, box in enumerate((mkb, mvb)):
            found = mem_in[:, blk, kind].reshape(seq_count * capacity, half)
            found = matmul(spots[blk], found, TN).astype(jnp.bfloat16)
            for head in range(HALF):
                box[blk, head] = found[:, head * HEAD_DIM : (head + 1) * HEAD_DIM]

    def blend(pieces):
        top = functools.reduce(jnp.maximum, [level for _, level in pieces])
        total, mixed = 0.0, 0.0
        for value, level in pieces:
            share = jnp.exp2(level - top)
            total = total + share
            mixed = mixed + value * share
        return mixed / total, top + jnp.log(total) * LOG2E

    def finish(i, carry):
        head, blk = i // 2, i % 2
        scores = matmul(mkb[blk, head], qb[blk, head], NT) * (SCALE * LOG2E)
        pieces = [(mixed_own[blk, head], lse[blk, head]), soften([(scores, mvb[blk, head])])]

        @pl.when(chip == 0)
        def _():
            mixed, lse[blk, head] = blend(pieces)
            ob[blk, head] = mixed.T.astype(jnp.bfloat16)

        @pl.when(chip == 1)
        def _():
            for copy in back_copy(blk, head):
                copy.wait_recv()
            far = (mixed_in[blk, head].astype(jnp.float32), lse_in[blk, head])
            mixed, lse[blk, head] = blend(pieces + [far])
            ob[blk, head] = mixed.T.astype(jnp.bfloat16)

        return carry

    lax.fori_loop(0, 2 * HALF, finish, 0)

    ends = []
    for head in range(HALF):
        ends.append(
            remote(ob.at[1 - core, head], attended.at[:, head_lanes(core, head)], end_sem.at[0, head], end_sem.at[1, head], mate)
        )
        ends.append(
            pltpu.make_async_copy(ob.at[core, head], attended.at[:, head_lanes(core, head)], end_sem.at[2, head])
        )
    for copy in ends:
        copy.start()
    for copy in ends:
        copy.wait()
    for away in range(1, seq_count):
        want_copy(away).wait_send()
        mem_copy(away).wait_send()

    @pl.when(chip == 0)
    def _():
        for head in range(HALF):
            for blk in range(2):
                for copy in back_copy(blk, head):
                    copy.wait_send()

    @pl.when(chip == 1)
    def _():
        for head in range(HALF):
            query_copy(head, True).wait_send()
            query_copy(head, False).wait_send()


def go_forward(limit, tokens, gain, projections, mem_keys, mem_values, wanted):
    block, width = tokens.shape
    mem_rows, topk = mem_keys.shape[0], wanted.shape[1]
    seq_count = lax.axis_size("seq")
    capacity = 2 * topk // seq_count
    slots = seq_count * capacity
    low, full = jnp.bfloat16, jnp.float32
    box = (2, HALF, block, HEAD_DIM)
    mem_box = (2, HALF, topk, HEAD_DIM)
    flat = (2, HALF, HEAD_DIM, block)
    row = (2, HALF, 1, block)
    mem = (seq_count, 2, 2, capacity, HALF * HEAD_DIM)
    dma = pltpu.SemaphoreType.DMA
    hbm, vmem = pl.BlockSpec(memory_space=pl.ANY), pl.BlockSpec(memory_space=pltpu.VMEM)
    struct = jax.ShapeDtypeStruct
    return pl.pallas_call(
        front_kernel,
        out_shape=(
            struct((block, width), low),
            struct(box, low), struct(box, low), struct(box, low), struct(box, low),
            struct(mem_box, low), struct(mem_box, low), struct(box, low), struct(row, full),
            struct((2, slots, topk), low), struct((mem_rows, slots), low),
        ),
        in_specs=[pl.BlockSpec(memory_space=pltpu.SMEM), hbm, vmem] + [hbm] * 6,
        out_specs=(hbm,) + (vmem,) * 10,
        scratch_shapes=[
            pltpu.VMEM((block, width), low), pltpu.VMEM((3, width, width), low), pltpu.VMEM((block, width), low),
            pltpu.VMEM((3, block, width), low), pltpu.VMEM((2, mem_rows, width), low),
            pltpu.VMEM((seq_count, 1, topk), jnp.int32), pltpu.VMEM((slots, mem_rows), low),
            pltpu.VMEM(mem, low), pltpu.VMEM(mem, low),
            pltpu.VMEM(flat, full), pltpu.VMEM(flat, low), pltpu.VMEM(flat, low),
            pltpu.VMEM(row, full), pltpu.VMEM(row, full),
            dma((7,)), dma((seq_count - 1,)), dma((seq_count - 1,)), dma((seq_count - 1,)), dma((seq_count - 1,)), dma((1,)),
            dma((3, HALF)), dma((3, HALF)), dma((3, HALF)),
            dma((2, HALF)), dma((2, HALF)), dma((2, 2, HALF)), dma((2, 2, HALF)), dma((3, HALF)),
        ],
        name="go_forward",
        compiler_params=pltpu.CompilerParams(collective_id=4, has_side_effects=True, vmem_limit_bytes=56 * 2**20),
    )(limit, tokens, gain, *projections, mem_keys, mem_values, wanted)


ALONG = (("x", "y", "low", "high"), ("y", "x", "low", "high"), ("low", "high", "y", "x"), ("low", "high", "x", "y"))
TURNS = (1, 1, 3, 3, 1, 1, 2, 3, 0, 1, 0, 1, 1, 3, 3, 0, 1, 0, 0, 1, 2, 1, 2, 2, 2, 2, 3, 1, 1, 3, 1, 1, 3, 0, 1, 1, 0, 2, 2, 1, 1, 2)
PLAN = (
    (),
    ((0, 0), (1, 0),),
    ((2, 0), (3, 0),),
    ((0, 1), (4, 0), (5, 0),),
    ((1, 1), (2, 1), (6, 0), (7, 0), (0, 2),),
    ((3, 1), (4, 1), (8, 0), (9, 0), (1, 2),),
    ((5, 1), (10, 0), (11, 0), (6, 1), (2, 2), (4, 2),),
    ((9, 1), (12, 0), (7, 1), (13, 0), (8, 1), (0, 3), (5, 2),),
    ((11, 1), (1, 3), (14, 0), (15, 0), (10, 1), (4, 3), (3, 2), (2, 3),),
    ((12, 1), (16, 0), (9, 2), (17, 0), (8, 2), (6, 2), (11, 2), (10, 2), (2, 4), (13, 1),),
    ((18, 0), (5, 3), (19, 0), (7, 2), (15, 1), (0, 4), (3, 3), (1, 4), (16, 1), (12, 2), (14, 1),),
    ((6, 3), (20, 0), (9, 3), (21, 0),),
    ((8, 3), (4, 4), (11, 3), (17, 1), (10, 3), (19, 1),),
    ((15, 2), (3, 4), (18, 1), (12, 3),),
    ((7, 3), (16, 2), (13, 2), (6, 4), (21, 1), (5, 4),),
    (),
    ((19, 2), (17, 2), (22, 0), (20, 1),),
    (),
    ((23, 0), (18, 2), (14, 2), (7, 4), (24, 0), (15, 3), (9, 4), (25, 0),),
    ((8, 4), (16, 3), (11, 4), (19, 3),),
    ((10, 4), (17, 3), (12, 4),),
    ((13, 3),),
    (),
    ((22, 1), (21, 2), (38, 0), (14, 3), (13, 4),),
    (),
    ((39, 0), (14, 4),),
    ((23, 1), (20, 2), (18, 3), (40, 0), (24, 1),),
    (),
    ((41, 0), (15, 4), (25, 1),),
    (),
    ((39, 1), (16, 4), (20, 3), (19, 4), (21, 3), (17, 4),),
    (),
    ((22, 2),),
    (),
    ((40, 1), (39, 2), (38, 1), (20, 4),),
    (),
    ((23, 2),),
    ((18, 4), (22, 3),),
    ((23, 3), (24, 2),),
    ((41, 1), (24, 3),),
    (),
    ((39, 3),),
    ((25, 2), (21, 4), (40, 2),),
    (),
    ((25, 3),),
    ((26, 0), (27, 0),),
    ((28, 0), (29, 0),),
    ((30, 0), (31, 0), (38, 2), (32, 0),),
    ((40, 3), (33, 0), (34, 0), (27, 1), (35, 0), (22, 4),),
    ((36, 0), (26, 1), (37, 0),),
    ((28, 1), (23, 4),),
    ((29, 1), (41, 2), (30, 1),),
    ((24, 4), (25, 4), (32, 1), (39, 4),),
    ((31, 1), (33, 1), (38, 3),),
    ((40, 4), (27, 2), (37, 1),),
    ((34, 1), (26, 2), (36, 1),),
    ((28, 2), (27, 3), (35, 1), (30, 2), (29, 2), (41, 3), (28, 3), (31, 2), (38, 4), (33, 2), (30, 3), (32, 2), (34, 2), (36, 2), (31, 3), (26, 3), (33, 3), (37, 2), (35, 2), (34, 3), (27, 4), (29, 3), (26, 4), (36, 3), (28, 4), (41, 4), (30, 4), (37, 3), (32, 3), (35, 3), (29, 4), (31, 4), (33, 4), (37, 4), (32, 4), (34, 4), (36, 4), (35, 4),),
)
OFFERED = (20, 22, 24, 26)
RING = 8
NARROW = 38
ROWS = (32, 88)


def taken(unit, level):
    return [(unit, level) in events for events in PLAN].index(True)


class Sums:
    def __init__(self, down, made, own, stages, sums, local_sem, send_sem, recv_sem, peers):
        self.down, self.made, self.own, self.stages, self.sums = down, made, own, stages, sums
        self.local_sem, self.send_sem, self.recv_sem = local_sem, send_sem, recv_sem
        self.peers = peers
        seq, doc = lax.axis_index("seq"), lax.axis_index("doc")
        self.bits = {
            "core": seq % 2,
            "x": (seq // 2) % 2,
            "y": (seq // 4) % 2,
            "low": doc % 2,
            "high": (doc // 2) % 2,
        }

    def core_copy(self, kind, index):
        if kind == 0:
            source = self.made.at[index % RING, :, :, 1 - self.bits["core"]]
        else:
            source = self.down.at[:, :, 1 - self.bits["core"], :, :, :, pl.ds(index * UNIT, UNIT)]
        return remote(
            source,
            self.stages[kind][0].at[index],
            self.send_sem[kind].at[0, index],
            self.recv_sem[kind].at[0, index],
            self.peers["core"],
        )

    def own_copy(self, index):
        return pltpu.make_async_copy(
            self.down.at[:, :, self.bits["core"], :, :, :, pl.ds(index * UNIT, UNIT)],
            self.own.at[index % 2],
            self.local_sem.at[index % 2],
        )

    def put(self, unit, value):
        pl.when(unit >= RING)(lambda: self.core_copy(0, jnp.maximum(unit - RING, 0)).wait_send())
        self.made[unit % RING] = value.astype(jnp.bfloat16).reshape(self.made.shape[1:])
        self.core_copy(0, unit).start()

    def offer_down(self, index):
        self.core_copy(1, index).start()
        if index < 2 or taken(NARROW + index - 2, 0) < OFFERED[index]:
            self.own_copy(index).start()

    def half(self, kind, index, order, level, mine):
        name = order[level]
        left = [axis for axis in ("y", "x", "high", "low") if axis not in order[:level]]
        side = self.bits[name] if mine else 1 - self.bits[name]
        return (index,) + (slice(None),) * left.index(name) + (side,)

    def copy(self, kind, index, order, level):
        return remote(
            self.stages[kind][level - 1].at[self.half(kind, index, order, level - 1, False)],
            self.stages[kind][level].at[index],
            self.send_sem[kind].at[level, index],
            self.recv_sem[kind].at[level, index],
            self.peers[order[level - 1]],
        )

    def arrive(self, unit, level):
        kind = 0 if unit < NARROW else 1
        index = unit - kind * NARROW
        order = ALONG[TURNS[unit]]
        ref = self.stages[kind][level]
        if level == 0:
            self.core_copy(kind, index).wait_recv()
            if kind == 1:
                self.own_copy(index).wait()

            def add(i, carry):
                y, x = i // 2, i % 2
                mine = self.made[index % RING, y, x, self.bits["core"]] if kind == 0 else self.own[index % 2, y, x]
                ref[index, y, x] = ref[index, y, x] + mine
                return carry

            lax.fori_loop(0, 4, add, 0)
            if kind == 1 and index < 2 and taken(unit, 0) >= OFFERED[index + 2]:
                self.own_copy(index + 2).start()
        else:
            self.copy(kind, index, order, level).wait_recv()
            kept = self.stages[kind][level - 1][self.half(kind, index, order, level - 1, True)]
            if level < 4:
                ref[index] = ref[index] + kept
            else:
                self.sums[kind][index] = ref[index].astype(jnp.float32) + kept.astype(jnp.float32)
        if level < 4:
            self.copy(kind, index, order, level + 1).start()

    def run(self, place):
        for unit, level in PLAN[place]:
            self.arrive(unit, level)

    def run_turn(self, first, turn, count):
        for k in range(count):
            if PLAN[first + k]:
                pl.when(turn == k)(lambda: self.run(first + k))

    def drain(self):
        for kind, count in enumerate((NARROW, 4)):
            def one(index, carry):
                pl.when((kind == 1) | (index >= NARROW - RING))(lambda: self.core_copy(kind, index).wait_send())
                for level in range(1, 5):
                    self.copy(kind, index, ALONG[0], level).wait_send()
                return carry

            lax.fori_loop(0, count, one, 0)


def back_kernel(
    limit_ref, mixed_in, qb_in, kb_in, vb_in, qx_in, mkb_in, mvb_in, ob_in, lse_in0, spots_in,
    tokens, cotangent, w_query, w_key, w_value, w_out, w_gate, w_up, w_down, gain, gain_two,
    layer_out, grad_tokens, gate_rows, up_rows, query_rows, key_rows, value_rows, out_rows, down_rows, gains_out,
    mem_home, down, grad, middle_kept, grad_middle,
    gb, gx, lse, delta, lse_in, delta_in, dq_cross, dqkv, mem_in, gain_buf, made, own, *rest,
):
    stages = [rest[5 * c : 5 * c + 5] for c in range(2)]
    sums = rest[10:12]
    local_sem, send_sems, recv_sems, rest = rest[12], rest[13:15], rest[15:17], rest[17:]
    (
        in_sem, gb_local, gb_send, gb_recv, spot_sem, far_send, far_recv, row_send, row_recv, back_send, back_recv,
        mate_send, mate_recv, mem_local, mem_send, mem_recv, gain_send, gain_recv, load_sem, weight_sem, done_sem, front_sem, tile_sem, stage_sem,
    ) = rest
    core, chip, mate, across, diagonal = seats()
    seq, doc = lax.axis_index("seq"), lax.axis_index("doc")
    seq_count = mem_in.shape[0]
    block = grad.shape[0]
    limit = limit_ref[0]
    peers = {
        "core": mate,
        "x": across,
        "y": (flip(seq, 4), doc),
        "low": (seq, flip(doc, 1)),
        "high": (seq, flip(doc, 2)),
    }
    others = [(lax.rem(seq + away, seq_count), doc) for away in range(1, seq_count)]
    meet(others + [peers["low"], peers["high"]])
    engine = Sums(down, made, own, stages, sums, local_sem, send_sems, recv_sems, peers)

    def grad_copy(head, own):
        return remote(
            grad.at[:, head_lanes(core if own else 1 - core, head)],
            gx.at[core, head],
            far_send.at[0 if own else 1, head],
            far_recv.at[core, head],
            across if own else diagonal,
        )

    def arrived_grad(far, head):
        return remote(
            grad.at[:, head_lanes(core, head)], gx.at[far, head], far_send.at[0, head], far_recv.at[far, head], across
        )

    def row_copies():
        return (
            remote(lse, lse_in, row_send.at[0], row_recv.at[0], across),
            remote(delta, delta_in, row_send.at[1], row_recv.at[1], across),
        )

    def back_copy(blk, head):
        return remote(dq_cross.at[blk, head], dq_cross.at[blk, head], back_send.at[blk, head], back_recv.at[blk, head], across)

    def mate_copy(box, i, head):
        lanes = head_lanes(core, head)
        return remote(box.at[i, head], dqkv.at[i, :, lanes], mate_send.at[i, head], mate_recv.at[i, head], mate)

    def mate_arrival(i, head):
        lanes = head_lanes(1 - core, head)
        return remote(gb.at[0, head], dqkv.at[i, :, lanes], mate_send.at[i, head], mate_recv.at[i, head], mate)

    def mem_copy(box, away):
        peer = lax.rem(seq + away, seq_count)
        return remote(box.at[peer], mem_in.at[seq], mem_send.at[away - 1], mem_recv.at[away - 1], (peer, doc))

    def far_start(head):
        @pl.when(chip == 1)
        def _():
            grad_copy(head, True).start()
            grad_copy(head, False).start()

    def front(normed, normed_t, grad_y, total, back, hidden_t, mixed):
        width = total.shape[1]
        tiles = w_gate.shape[1] // UNIT
        part = 128
        copies = [
            pltpu.make_async_copy(mixed_in, mixed, front_sem.at[0]),
            pltpu.make_async_copy(cotangent, grad_y, front_sem.at[1]),
        ]
        for copy in copies:
            copy.start()

        def strip(i):
            return pl.ds(pl.multiple_of(i * UNIT, UNIT), UNIT)

        def chunk(i):
            return pl.ds(pl.multiple_of(i * part, part), part)

        def opening(rows, weights, middle):
            loads = [
                pltpu.make_async_copy(tokens, rows, front_sem.at[2]),
                pltpu.make_async_copy(w_out, weights, front_sem.at[3]),
            ]
            for copy in loads:
                copy.start()
            for copy in copies + loads:
                copy.wait()

            def join(j, carry):
                middle[:, strip(j)] = rows[:, strip(j)].astype(jnp.float32) + matmul(mixed[...], weights[:, strip(j)], NN)
                return carry

            lax.fori_loop(0, width // UNIT, join, 0)
            keep = pltpu.make_async_copy(middle, middle_kept, front_sem.at[4])
            keep.start()

            def norm(i, carry):
                x = middle[chunk(i), :]
                factor = lax.rsqrt(jnp.mean(x * x, axis=-1, keepdims=True) + EPS)
                value = x * factor * gain_two[...]
                normed[chunk(i), :] = value.astype(jnp.bfloat16)
                normed_t[:, chunk(i)] = value.T.astype(jnp.bfloat16)
                total[chunk(i), :] = jnp.zeros((part, width), jnp.float32)
                back[chunk(i), :] = jnp.zeros((part, width), jnp.float32)
                return carry

            lax.fori_loop(0, block // part, norm, 0)
            keep.wait()

        pl.run_scoped(
            opening,
            pltpu.VMEM(tokens.shape, jnp.bfloat16), pltpu.VMEM(w_out.shape, jnp.bfloat16), pltpu.VMEM(total.shape, jnp.float32),
        )

        def hidden_units(w_in, w_back):
            def loads(tile):
                slot = tile % 2
                return (
                    pltpu.make_async_copy(w_gate.at[:, strip(tile)], w_in.at[slot, 0], tile_sem.at[slot, 0]),
                    pltpu.make_async_copy(w_up.at[:, strip(tile)], w_in.at[slot, 1], tile_sem.at[slot, 1]),
                    pltpu.make_async_copy(w_down.at[strip(tile), :], w_back.at[slot], tile_sem.at[slot, 2]),
                )

            for copy in loads(0):
                copy.start()

            def one(tile, carry):
                slot = tile % 2

                @pl.when(tile + 1 < tiles)
                def _():
                    for copy in loads(tile + 1):
                        copy.start()

                for copy in loads(tile):
                    copy.wait()
                opened = matmul(normed[...], w_in[slot, 0], NN)
                upper = matmul(normed[...], w_in[slot, 1], NN)
                sigma = 1.0 / (1.0 + jnp.exp(-opened))
                gated = opened * sigma
                hidden = gated * upper
                total[...] += matmul(hidden.astype(jnp.bfloat16), w_back[slot], NN)
                hidden_t[strip(tile), :] = hidden.T.astype(jnp.bfloat16)
                grad_hidden = matmul(grad_y[...], w_back[slot], NT)
                grad_opened = (grad_hidden * upper * sigma * (1.0 + opened * (1.0 - sigma))).astype(jnp.bfloat16)
                grad_upper = (grad_hidden * gated).astype(jnp.bfloat16)
                back[...] += matmul(grad_opened, w_in[slot, 0], NT) + matmul(grad_upper, w_in[slot, 1], NT)
                for kind, value in enumerate((grad_opened, grad_upper)):
                    engine.put(2 * tile + kind, matmul(normed_t[...], value, NN))
                engine.run_turn(0, tile, tiles)
                return carry

            lax.fori_loop(0, tiles, one, 0)

        pl.run_scoped(
            hidden_units,
            pltpu.VMEM((2, 2, width, UNIT), jnp.bfloat16), pltpu.VMEM((2, UNIT, width), jnp.bfloat16),
        )

        def closing(middle, weights, branch, branch_back, stage_down):
            loads = [
                pltpu.make_async_copy(middle_kept, middle, front_sem.at[2]),
                pltpu.make_async_copy(w_out, weights, front_sem.at[3]),
            ]
            for copy in loads:
                copy.start()
            engine.run(11)
            for copy in loads:
                copy.wait()

            def norm_back(i, carry):
                x = middle[chunk(i), :]
                factor = lax.rsqrt(jnp.mean(x * x, axis=-1, keepdims=True) + EPS)
                unit = x * factor
                grad_normed = back[chunk(i), :]
                normed[chunk(i), :] = (x + total[chunk(i), :]).astype(jnp.bfloat16)
                scaled = gain_two[...] * grad_normed
                inner = jnp.mean(scaled * unit, axis=-1, keepdims=True)
                value = grad_y[chunk(i), :].astype(jnp.float32) + factor * (scaled - unit * inner)
                middle[chunk(i), :] = value
                branch[chunk(i), :] = value.astype(jnp.bfloat16)
                return carry + jnp.sum(grad_normed * unit, axis=0, keepdims=True)

            gain_buf[0, 0, 1] = lax.fori_loop(0, block // part, norm_back, jnp.zeros((1, width), jnp.float32))
            writes = [
                pltpu.make_async_copy(normed, layer_out, front_sem.at[0]),
                pltpu.make_async_copy(middle, grad_middle, front_sem.at[2]),
            ]
            for copy in writes:
                copy.start()

            engine.run(12)

            def to_attended(j, carry):
                branch_back[:, strip(j)] = matmul(branch[...], weights[strip(j), :], NT).astype(jnp.bfloat16)
                return carry

            lax.fori_loop(0, width // UNIT, to_attended, 0)
            store = pltpu.make_async_copy(branch_back, grad, front_sem.at[1])
            store.start()
            engine.run(13)
            store.wait()
            far_start(0)
            share_heads((grad,), (gb,), core, mate, gb_local, gb_send, gb_recv)

            def turn_over(i, carry):
                normed_t[:, chunk(i)] = mixed[chunk(i), :].astype(jnp.float32).T.astype(jnp.bfloat16)
                return carry

            lax.fori_loop(0, block // part, turn_over, 0)

            for j in range(4):
                engine.put(jnp.int32(22 + j), matmul(normed_t[...], branch[:, j * UNIT : (j + 1) * UNIT], NN))
                engine.run(14 + j)
            deep = stage_down.shape[4]
            tall = 8 * deep

            def down_store(n):
                i = n % 4
                return pltpu.make_async_copy(
                    stage_down.at[n % 2], down.at[i // 2, i % 2, :, :, :, :, strip(n // 4)], stage_sem.at[n % 2]
                )

            def down_part(n):
                i, j = n % 4, n // 4
                value = matmul(hidden_t[pl.ds(pl.multiple_of(i * tall, 64), tall), :], grad_y[:, strip(j)], NN)
                pl.when(n > 1)(lambda: down_store(n - 2).wait())
                for k in range(8):
                    stage_down[n % 2, k // 4, (k // 2) % 2, k % 2] = value[k * deep : (k + 1) * deep].astype(jnp.bfloat16)
                down_store(n).start()

            def down_parts(m, carry):
                down_part(2 * m)
                down_part(2 * m + 1)
                for j in range(3):
                    pl.when(m == 2 * j + 2)(lambda: engine.offer_down(j))
                pl.when(m == 1)(lambda: far_start(1))
                pl.when(m == 4)(lambda: far_start(2))
                engine.run_turn(18, m, 8)
                return carry

            lax.fori_loop(0, 8, down_parts, 0)
            down_store(14).wait()
            down_store(15).wait()
            engine.offer_down(3)
            far_start(3)
            for copy in writes:
                copy.wait()

        pl.run_scoped(
            closing,
            pltpu.VMEM(total.shape, jnp.float32), pltpu.VMEM(w_out.shape, jnp.bfloat16),
            pltpu.VMEM(normed.shape, jnp.bfloat16), pltpu.VMEM(normed.shape, jnp.bfloat16),
            pltpu.VMEM((2, 2, 2, 2, ROWS[1], UNIT), jnp.bfloat16),
        )

    pl.run_scoped(
        front,
        pltpu.VMEM(tokens.shape, jnp.bfloat16), pltpu.VMEM((tokens.shape[1], block), jnp.bfloat16),
        pltpu.VMEM(tokens.shape, jnp.bfloat16), pltpu.VMEM(tokens.shape, jnp.float32), pltpu.VMEM(tokens.shape, jnp.float32),
        pltpu.VMEM((w_gate.shape[1], block), jnp.bfloat16), pltpu.VMEM(tokens.shape, jnp.bfloat16),
    )

    def attention(qb, kb, vb, qx, mkb, mvb, ob, dq_own, dk_sum, dv_sum, dm, dqkv_mate, mem_out, spots):
        inputs = [
            pltpu.make_async_copy(src, dst, in_sem.at[i])
            for i, (src, dst) in enumerate(
                ((qb_in, qb), (kb_in, kb), (vb_in, vb), (mkb_in, mkb), (mvb_in, mvb), (ob_in, ob), (lse_in0, lse), (qx_in, qx))
            )
        ]
        spot_copies = [pltpu.make_async_copy(spots_in, spots, spot_sem.at[0])]
        for copy in inputs + spot_copies:
            copy.start()
        for head in range(HALF):
            remote(grad.at[:, head_lanes(core, head)], gb.at[core, head], gb_send.at[0, head], gb_recv.at[0, head], mate).wait()
            pltpu.make_async_copy(grad.at[:, head_lanes(core, head)], gb.at[core, head], gb_local.at[0, head]).wait()
        for copy in inputs + spot_copies:
            copy.wait()
        engine.run(26)

        def rows(i, carry):
            head, blk = i // 2, i % 2
            product = gb[blk, head].astype(jnp.float32) * ob[blk, head].astype(jnp.float32)
            delta[blk, head] = jnp.sum(product.T, axis=0, keepdims=True)
            return carry

        lax.fori_loop(0, 2 * HALF, rows, 0)

        @pl.when(chip == 1)
        def _():
            for copy in row_copies():
                copy.start()

        def pull(key_rows, value_rows, query, grad_rows, level, inner, where):
            scores = matmul(key_rows, query, NT) * (SCALE * LOG2E)
            if where is not None:
                scores = masked(scores, where[0], limit, where[1])
            weights = jnp.exp2(scores - level)
            grad_weights = matmul(value_rows, grad_rows, NT)
            grad_scores = (weights * (grad_weights - inner)).astype(jnp.bfloat16)
            return (
                matmul(grad_scores, query, NN),
                matmul(weights.astype(jnp.bfloat16), grad_rows, NN),
                matmul(key_rows, grad_scores, TN),
            )

        def own_head(head, carry):
            lanes = pl.ds(pl.multiple_of(head * HEAD_DIM, HEAD_DIM), HEAD_DIM)
            for blk in range(2):
                query, grad_rows = qb[blk, head], gb[blk, head]
                level, inner = lse[blk, head], delta[blk, head]
                total = 0.0
                for kblk in range(blk + 1):
                    gk, gv, gq = pull(
                        kb[kblk, head], vb[kblk, head], query, grad_rows, level, inner,
                        ((2 * chip + kblk) * block, kblk == blk),
                    )
                    if kblk == blk:
                        dk_sum[kblk, head], dv_sum[kblk, head] = gk, gv
                    else:
                        dk_sum[kblk, head] += gk
                        dv_sum[kblk, head] += gv
                    total = total + gq
                gk, gv, gq = pull(mkb[blk, head], mvb[blk, head], query, grad_rows, level, inner, None)
                dm[blk, 0, :, lanes] = (gk * SCALE).astype(jnp.bfloat16)
                dm[blk, 1, :, lanes] = gv.astype(jnp.bfloat16)
                dq_own[blk, head] = total + gq
            engine.run_turn(27, head, HALF)
            return carry

        lax.fori_loop(0, HALF, own_head, 0)

        for blk in range(2):
            for kind in range(2):
                rows_out = matmul(spots[blk], dm[blk, kind], NN).astype(jnp.bfloat16)
                mem_out[:, blk, kind] = rows_out.reshape(mem_out.shape[0], mem_out.shape[3], mem_out.shape[4])
        for away in range(1, seq_count):
            mem_copy(mem_out, away).start()
        own_rows = pltpu.make_async_copy(mem_out.at[seq], mem_in.at[seq], mem_local.at[0])
        own_rows.start()
        engine.run(31)

        @pl.when(chip == 0)
        def _():
            for copy in row_copies():
                copy.wait_recv()

        def far_turn(i, carry):
            head, blk = i // 2, i % 2

            @pl.when(chip == 0)
            def _():
                arrived_grad(blk, head).wait_recv()
                query, grad_rows = qx[blk, head], gx[blk, head]
                level, inner = lse_in[blk, head], delta_in[blk, head]
                total = 0.0
                for kblk in range(2):
                    gk, gv, gq = pull(
                        kb[kblk, head], vb[kblk, head], query, grad_rows, level, inner, (kblk * block, False)
                    )
                    dk_sum[kblk, head] += gk
                    dv_sum[kblk, head] += gv
                    total = total + gq
                dq_cross[blk, head] = total.astype(jnp.bfloat16)
                back_copy(blk, head).start()

            engine.run_turn(32, i, 2 * HALF)

            @pl.when(chip == 1)
            def _():
                back_copy(blk, head).wait_recv()
                dq_own[blk, head] += dq_cross[blk, head].astype(jnp.float32)

            return carry

        lax.fori_loop(0, 2 * HALF, far_turn, 0)

        def results(blk, head):
            return (
                (dq_own[blk, head].T * SCALE).astype(jnp.bfloat16),
                (dk_sum[blk, head] * SCALE).astype(jnp.bfloat16),
                dv_sum[blk, head].astype(jnp.bfloat16),
            )

        def for_mate(head, carry):
            for i, value in enumerate(results(1 - core, head)):
                dqkv_mate[i, head] = value
                mate_copy(dqkv_mate, i, head).start()
            return carry

        def for_own(head, carry):
            for i, value in enumerate(results(core, head)):
                dqkv[i, :, head_lanes(core, head)] = value
            return carry

        lax.fori_loop(0, HALF, for_mate, 0)
        engine.run(40)
        lax.fori_loop(0, HALF, for_own, 0)
        engine.run(41)
        for away in range(1, seq_count):
            mem_copy(mem_out, away).wait_send()
        own_rows.wait()
        for i in range(3):
            for head in range(HALF):
                mate_copy(dqkv_mate, i, head).wait_send()

    box = (2, HALF, block, HEAD_DIM)
    mem_box = mkb_in.shape
    low, full = jnp.bfloat16, jnp.float32
    pl.run_scoped(
        attention,
        pltpu.VMEM(box, low), pltpu.VMEM(box, low), pltpu.VMEM(box, low), pltpu.VMEM(box, low),
        pltpu.VMEM(mem_box, low), pltpu.VMEM(mem_box, low), pltpu.VMEM(box, low),
        pltpu.VMEM((2, HALF, HEAD_DIM, block), full), pltpu.VMEM(box, full), pltpu.VMEM(box, full),
        pltpu.VMEM((2, 2, mem_box[2], HALF * HEAD_DIM), low),
        pltpu.VMEM((3, HALF, block, HEAD_DIM), low), pltpu.VMEM(mem_in.shape, low), pltpu.VMEM(spots_in.shape, low),
    )

    def tail(normed, dx, middle, rows, weights):
        width = dx.shape[1]
        chunk = weights.shape[2]
        loads = [
            pltpu.make_async_copy(tokens, rows, load_sem.at[1]),
            pltpu.make_async_copy(grad_middle, middle, load_sem.at[2]),
        ]

        def weight_copies(j):
            at = pl.ds(pl.multiple_of(j * chunk, chunk), chunk)
            return [
                pltpu.make_async_copy(w.at[at, :], weights.at[j % 2, i], weight_sem.at[j % 2, i])
                for i, w in enumerate((w_query, w_key, w_value))
            ]

        for copy in loads + weight_copies(0):
            copy.start()
        loads[0].wait()
        part = 64

        def norm(i, carry):
            at = pl.ds(pl.multiple_of(i * 2 * part, 2 * part), 2 * part)
            x = rows[at, :].astype(jnp.float32)
            factor = lax.rsqrt(jnp.mean(x * x, axis=-1, keepdims=True) + EPS)
            normed[:, at] = (x * factor * gain[...]).T.astype(jnp.bfloat16)
            return carry

        lax.fori_loop(0, block // (2 * part), norm, 0)
        for i in range(3):
            for head in range(HALF):
                mate_arrival(i, head).wait_recv()
        engine.run(42)

        def make(w):
            lanes = pl.ds(pl.multiple_of(lax.rem(w, 4) * UNIT, UNIT), UNIT)
            engine.put(26 + w, matmul(normed[...], dqkv[w // 4, :, lanes], NN))

        def build(j, carry):
            make(2 * j)
            make(2 * j + 1)
            engine.run_turn(43, j, 6)
            return carry

        lax.fori_loop(0, 6, build, 0)

        def input_part(j, carry):
            for copy in weight_copies(j):
                copy.wait()

            @pl.when(j < 3)
            def _():
                for copy in weight_copies(j + 1):
                    copy.start()

            total = 0.0
            for i in range(3):
                total = total + matmul(dqkv[i], weights[j % 2, i], NT)
            dx[:, pl.ds(pl.multiple_of(j * chunk, chunk), chunk)] = total
            engine.run_turn(49, j, 4)
            return carry

        lax.fori_loop(0, 4, input_part, 0)
        loads[1].wait()

        def norm_back(i, carry):
            at = pl.ds(pl.multiple_of(i * part, part), part)
            x = rows[at, :].astype(jnp.float32)
            factor = lax.rsqrt(jnp.mean(x * x, axis=-1, keepdims=True) + EPS)
            unit = x * factor
            grad_normed = dx[at, :]
            scaled = gain[...] * grad_normed
            inner = jnp.mean(scaled * unit, axis=-1, keepdims=True)
            rows[at, :] = (middle[at, :] + factor * (scaled - unit * inner)).astype(jnp.bfloat16)
            return carry + jnp.sum(grad_normed * unit, axis=0, keepdims=True)

        gain_buf[0, 0, 0] = lax.fori_loop(0, block // part, norm_back, jnp.zeros((1, width), jnp.float32))
        out_copy = pltpu.make_async_copy(rows, grad_tokens, load_sem.at[1])
        out_copy.start()

        def gain_copy(level):
            name = ("core", "x", "y", "low", "high")[level]
            return remote(
                gain_buf.at[0, level], gain_buf.at[1, level], gain_send.at[level], gain_recv.at[level], peers[name]
            )

        gain_copy(0).start()
        engine.run(53)
        for away in range(1, seq_count):
            source = lax.rem(seq + seq_count - away, seq_count)
            remote(mem_in.at[source], mem_in.at[source], mem_send.at[away - 1], mem_recv.at[away - 1], (source, doc)).wait_recv()
        mem_copy_out = pltpu.make_async_copy(mem_in, mem_home, load_sem.at[2])
        mem_copy_out.start()
        engine.run(54)
        engine.run(55)
        events = PLAN[56]
        stops = [len(events) * k // 6 for k in range(1, 6)]
        for n, (unit, level) in enumerate(events):
            for step in range(5):
                if n == stops[step]:
                    gain_copy(step).wait_recv()
                    total = gain_buf[0, step] + gain_buf[1, step]
                    if step < 4:
                        gain_buf[0, step + 1] = total
                        gain_copy(step + 1).start()
                    else:
                        gains_out[...] = total
            engine.arrive(unit, level)
        homes = []
        for u in range(11):
            homes += [(0, 2 * u, gate_rows, u), (0, 2 * u + 1, up_rows, u)]
        for j in range(4):
            homes += [(0, 22 + j, out_rows, j), (0, 26 + j, query_rows, j), (0, 30 + j, key_rows, j), (0, 34 + j, value_rows, j)]
            homes.append((1, j, down_rows, j))
        outs = []
        for i, (kind, unit, ref, place) in enumerate(homes):
            outs.append(
                pltpu.make_async_copy(sums[kind].at[unit], ref.at[:, pl.ds(place * UNIT, UNIT)], done_sem.at[i])
            )
            outs[-1].start()
        engine.drain()
        for level in range(5):
            gain_copy(level).wait_send()
        for copy in outs + [out_copy, mem_copy_out]:
            copy.wait()

    width = w_query.shape[0]
    pl.run_scoped(
        tail,
        pltpu.VMEM((width, block), low),
        pltpu.VMEM((block, width), full), pltpu.VMEM((block, width), full), pltpu.VMEM((block, width), low),
        pltpu.VMEM((2, 3, UNIT, width), low),
    )

    @pl.when(chip == 0)
    def _():
        for head in range(HALF):
            for blk in range(2):
                back_copy(blk, head).wait_send()

    @pl.when(chip == 1)
    def _():
        for copy in row_copies():
            copy.wait_send()
        for head in range(HALF):
            grad_copy(head, True).wait_send()
            grad_copy(head, False).wait_send()


def go_back(limit, attended, saved, tokens, cotangent, weights, gain, gain_two):
    block, width = tokens.shape
    low, full = jnp.bfloat16, jnp.float32
    box = (2, HALF, block, HEAD_DIM)
    row = (2, HALF, 1, block)
    seq_count = lax.axis_size("seq")
    capacity = 2 * TOPK // seq_count
    dma = pltpu.SemaphoreType.DMA
    hbm, vmem = pl.BlockSpec(memory_space=pl.ANY), pl.BlockSpec(memory_space=pltpu.VMEM)
    struct = jax.ShapeDtypeStruct
    ff = weights[4].shape[1]
    *saved, picked_t = saved
    spots = saved[8]

    def wide(rows, columns):
        return struct((2, 2, 2, 2, 2, rows, columns), low)

    mem = (seq_count, 2, 2, capacity, HALF * HEAD_DIM)
    units = (NARROW, 4)
    scratch = [
        pltpu.VMEM(box, low), pltpu.VMEM(box, low),
        pltpu.VMEM(row, full), pltpu.VMEM(row, full), pltpu.VMEM(row, full), pltpu.VMEM(row, full),
        pltpu.VMEM((2, HALF, HEAD_DIM, block), low),
        pltpu.VMEM((3, block, width), low), pltpu.VMEM(mem, low),
        pltpu.VMEM((2, 5, 2, 1, width), full),
        pltpu.VMEM((RING, 2, 2, 2, 2, 2, ROWS[0], UNIT), low),
        pltpu.VMEM((2, 2, 2, 2, 2, ROWS[1], UNIT), low),
    ]
    for c in range(2):
        scratch += [pltpu.VMEM((units[c],) + (2,) * k + (ROWS[c], UNIT), low) for k in (4, 3, 2, 1, 0)]
    scratch += [pltpu.VMEM((units[c], ROWS[c], UNIT), full) for c in range(2)]
    scratch += [dma((2,))]
    scratch += [dma((5, units[c])) for c in range(2)] * 2
    scratch += [
        dma((8,)), dma((1, HALF)), dma((1, HALF)), dma((1, HALF)), dma((1,)),
        dma((2, HALF)), dma((2, HALF)), dma((2,)), dma((2,)), dma((2, HALF)), dma((2, HALF)),
        dma((3, HALF)), dma((3, HALF)), dma((1,)), dma((seq_count - 1,)), dma((seq_count - 1,)),
        dma((5,)), dma((5,)), dma((4,)), dma((2, 3)), dma((sum(units),)),
        dma((5,)), dma((2, 3)), dma((2,)),
    ]
    rows = struct((32, width), full)
    mem_rows = picked_t.shape[0]
    results = pl.pallas_call(
        back_kernel,
        out_shape=(
            struct((block, width), low), struct((block, width), low),
            struct((32, ff), full), struct((32, ff), full),
            rows, rows, rows, rows,
            struct((88, width), full), struct((2, 1, width), full),
            struct(mem, low),
            wide(88, width),
            struct((block, width), low), struct((block, width), full), struct((block, width), full),
        ),
        in_specs=[pl.BlockSpec(memory_space=pltpu.SMEM)] + [hbm] * 19 + [vmem] * 2,
        out_specs=(hbm,) * 9 + (vmem,) + (hbm,) * 5,
        scratch_shapes=scratch,
        name="go_back",
        compiler_params=pltpu.CompilerParams(collective_id=3, has_side_effects=True, vmem_limit_bytes=60 * 2**20),
    )(limit, attended, *saved, tokens, cotangent, *weights, gain, gain_two)
    return deliver(results[:9], results[10], picked_t) + (results[9],)


def deliver_kernel(*refs):
    sources, mem_home, picked_t = refs[:9], refs[9], refs[10]
    targets, tables = refs[11:20], refs[20:22]
    boxes, rest = refs[22:31], refs[31:]
    rows, pick, table, in_sem, out_sem, load_sem, table_sem = rest
    loads = [
        pltpu.make_async_copy(mem_home, rows, load_sem.at[0]),
        pltpu.make_async_copy(picked_t, pick, load_sem.at[1]),
    ]
    ins = [pltpu.make_async_copy(a, b, in_sem.at[i]) for i, (a, b) in enumerate(zip(sources, boxes))]
    outs = [pltpu.make_async_copy(a, b, out_sem.at[i]) for i, (a, b) in enumerate(zip(boxes, targets))]
    for copy in loads + ins:
        copy.start()
    for copy in loads:
        copy.wait()
    half = rows.shape[4]
    stores = []
    for kind in range(2):
        for side in range(2):
            values = jnp.concatenate(
                [rows[2 * src + side, blk, kind] for src in range(rows.shape[0] // 2) for blk in range(2)], axis=0
            )
            table[2 * kind + side] = matmul(pick[...], values, NN)
            stores.append(
                pltpu.make_async_copy(
                    table.at[2 * kind + side],
                    tables[kind].at[:, side * half : (side + 1) * half],
                    table_sem.at[2 * kind + side],
                )
            )
            stores[-1].start()
    for arrived, left in zip(ins, outs):
        arrived.wait()
        left.start()
    for copy in stores + outs:
        copy.wait()


def deliver(arrays, mem_home, picked_t):
    struct = jax.ShapeDtypeStruct
    hbm = pl.BlockSpec(memory_space=pl.ANY)
    mem_rows, half = picked_t.shape[0], mem_home.shape[4]
    table = struct((mem_rows, 2 * half), jnp.float32)
    return tuple(
        pl.pallas_call(
            deliver_kernel,
            out_shape=tuple(struct(a.shape, a.dtype) for a in arrays) + (table, table),
            in_specs=[hbm] * 11,
            out_specs=(hbm,) * 11,
            scratch_shapes=[pltpu.VMEM(a.shape, a.dtype) for a in arrays] + [
                pltpu.VMEM(mem_home.shape, jnp.bfloat16), pltpu.VMEM(picked_t.shape, jnp.bfloat16),
                pltpu.VMEM((4, mem_rows, half), jnp.float32),
                pltpu.SemaphoreType.DMA((9,)), pltpu.SemaphoreType.DMA((9,)), pltpu.SemaphoreType.DMA((2,)), pltpu.SemaphoreType.DMA((4,)),
            ],
            name="deliver",
            compiler_params=pltpu.CompilerParams(vmem_limit_bytes=60 * 2**20),
        )(*arrays, mem_home, picked_t)
    )


def rms_factor(values):
    return lax.rsqrt(jnp.mean(values * values, axis=-1, keepdims=True) + EPS)


def dot32(left, right):
    return jnp.dot(left, right, preferred_element_type=jnp.float32)


def fitting():
    return (lax.axis_size("seq"), lax.axis_size("doc")) == (8, 4)


def exchange(rows, owner_count, capacity):
    parts, _, width = rows.shape
    shaped = rows.reshape(parts, owner_count, capacity, width)
    moved = lax.all_to_all(shaped, "seq", split_axis=1, concat_axis=1, tiled=True)
    return moved.reshape(parts, owner_count * capacity, width)


def on_device(
    tokens,
    cotangent,
    attn_gain,
    w_query,
    w_key,
    w_value,
    w_out,
    ffn_gain,
    w_gate,
    w_up,
    w_down,
    mem_keys,
    mem_values,
    seg_len,
    mem_idx,
):
    low = jnp.bfloat16
    stream_count, block_len, model_width = tokens.shape
    mem_rows = mem_keys.shape[1]
    seq_count = lax.axis_size("seq")
    segment = lax.axis_index("seq") // BPS
    capacity = 2 * TOPK // seq_count
    slot_count = seq_count * capacity
    limit = lax.dynamic_index_in_dim(seg_len, segment, 1, keepdims=False)

    gain_one = attn_gain.astype(jnp.float32)
    gain_two = ffn_gain.astype(jnp.float32)
    if fitting():
        attended, *saved = go_forward(
            limit, tokens[0], gain_one[None], (w_query, w_key, w_value), mem_keys[0], mem_values[0], mem_idx[0]
        )
        layer_out, grad_tokens, gate_rows, up_rows, query_rows, key_rows, value_rows, out_rows, down_rows, grad_mk, grad_mv, gains = go_back(
            limit,
            attended,
            saved,
            tokens[0],
            cotangent[0],
            (w_query, w_key, w_value, w_out, w_gate, w_up, w_down),
            gain_one[None],
            gain_two[None],
        )
        index = lax.axis_index("seq") * lax.axis_size("doc") + lax.axis_index("doc")
        parts = gains.reshape(2, seq_count * lax.axis_size("doc"), -1)
        attn_row, ffn_row = lax.dynamic_index_in_dim(parts, index, 1, keepdims=False)
        return (
            layer_out[None],
            grad_tokens[None],
            attn_row,
            query_rows,
            key_rows,
            value_rows,
            out_rows,
            ffn_row,
            gate_rows,
            up_rows,
            down_rows,
            grad_mk[None],
            grad_mv[None],
        )

    tokens_f = tokens[0].astype(jnp.float32)
    factor_one = rms_factor(tokens_f)
    unit_one = tokens_f * factor_one
    normed_one = (unit_one * gain_one).astype(low)
    chosen = mem_idx[0, 0]
    owner = chosen // mem_rows
    order = jnp.arange(TOPK)
    same_before = (owner[:, None] == owner[None, :]) & (order[None, :] < order[:, None])
    slot = owner * capacity + jnp.sum(same_before.astype(jnp.int32), axis=1)
    placed = slot[:, None] == jnp.arange(slot_count)[None, :]
    request = jnp.sum(jnp.where(placed, (chosen % mem_rows)[:, None] + 1, 0), axis=0) - 1
    requested = lax.all_to_all(
        request.reshape(seq_count, capacity), "seq", split_axis=0, concat_axis=0, tiled=True
    ).reshape(slot_count)
    picked = (requested[:, None] == jnp.arange(mem_rows)[None, :]).astype(low)
    placed = placed.astype(low)
    sent = jnp.stack((dot32(picked, mem_keys[0]).astype(low), dot32(picked, mem_values[0]).astype(low)))
    arrived = exchange(sent, seq_count, capacity)
    mem_key_rows = dot32(placed, arrived[0]).astype(low)
    mem_value_rows = dot32(placed, arrived[1]).astype(low)
    queries = dot32(normed_one, w_query).astype(low)
    keys = dot32(normed_one, w_key).astype(low)
    values = dot32(normed_one, w_value).astype(low)
    attended, *saved = attend_forward(limit, queries, keys, values, mem_key_rows, mem_value_rows)
    middle = tokens_f + dot32(attended, w_out)
    factor_two = rms_factor(middle)
    unit_two = middle * factor_two
    normed_two = (unit_two * gain_two).astype(low)
    gate = dot32(normed_two, w_gate)
    upper = dot32(normed_two, w_up)
    sigma = jax.nn.sigmoid(gate)
    hidden = (gate * sigma * upper).astype(low)
    layer_out = (middle + dot32(hidden, w_down)).astype(low)

    grad_y_low = cotangent[0]
    grad_y = grad_y_low.astype(jnp.float32)
    grad_down = dot32(hidden.T, grad_y_low)
    grad_hidden = dot32(grad_y_low, w_down.T)
    grad_gate_act = (grad_hidden * upper * sigma * (1.0 + gate * (1.0 - sigma))).astype(low)
    grad_up_act = (grad_hidden * gate * sigma).astype(low)
    grad_gate = dot32(normed_two.T, grad_gate_act)
    grad_up = dot32(normed_two.T, grad_up_act)
    grad_normed_two = dot32(grad_gate_act, w_gate.T) + dot32(grad_up_act, w_up.T)
    grad_ffn_gain = jnp.sum(grad_normed_two * unit_two, axis=0)
    scaled_two = gain_two * grad_normed_two
    grad_middle = grad_y + factor_two * (
        scaled_two - unit_two * jnp.mean(scaled_two * unit_two, axis=-1, keepdims=True)
    )
    grad_branch = grad_middle.astype(low)
    grad_out = dot32(attended.T, grad_branch)
    grad_attended = dot32(grad_branch, w_out.T).astype(low)
    grad_q, grad_k, grad_v, grad_mk, grad_mv = attend_backward(limit, grad_attended, saved)
    back = jnp.stack((dot32(placed.T, grad_mk).astype(low), dot32(placed.T, grad_mv).astype(low)))
    returned = exchange(back, seq_count, capacity)
    grad_mem_keys = dot32(picked.T, returned[0])
    grad_mem_values = dot32(picked.T, returned[1])
    grad_query = dot32(normed_one.T, grad_q)
    grad_key = dot32(normed_one.T, grad_k)
    grad_value = dot32(normed_one.T, grad_v)
    grad_normed_one = dot32(grad_q, w_query.T) + dot32(grad_k, w_key.T) + dot32(grad_v, w_value.T)
    grad_attn_gain = jnp.sum(grad_normed_one * unit_one, axis=0)
    scaled_one = gain_one * grad_normed_one
    grad_input = grad_middle + factor_one * (
        scaled_one - unit_one * jnp.mean(scaled_one * unit_one, axis=-1, keepdims=True)
    )
    grad_tokens = grad_input.astype(low)
    gate_rows, up_rows, query_rows, key_rows, value_rows, out_rows, down_rows, attn_row, ffn_row = [
        lax.psum_scatter(grad, ("seq", "doc"), scatter_dimension=0, tiled=True)
        for grad in (
            grad_gate, grad_up, grad_query, grad_key, grad_value, grad_out, grad_down, grad_attn_gain, grad_ffn_gain
        )
    ]
    return (
        layer_out[None],
        grad_tokens[None],
        attn_row,
        query_rows,
        key_rows,
        value_rows,
        out_rows,
        ffn_row,
        gate_rows,
        up_rows,
        down_rows,
        grad_mem_keys[None],
        grad_mem_values[None],
    )


def solution(mesh):
    in_specs = (
        P("doc", "seq", None),
        P("doc", "seq", None),
        P(),
        P(),
        P(),
        P(),
        P(),
        P(),
        P(),
        P(),
        P(),
        P("doc", "seq", None),
        P("doc", "seq", None),
        P("doc", None),
        P("doc", "seq", None),
    )
    out_specs = (
        P("doc", "seq", None),
        P("doc", "seq", None),
        P(("seq", "doc")),
        P(("seq", "doc"), None),
        P(("seq", "doc"), None),
        P(("seq", "doc"), None),
        P(("seq", "doc"), None),
        P(("seq", "doc")),
        P(("seq", "doc"), None),
        P(("seq", "doc"), None),
        P(("seq", "doc"), None),
        P("doc", "seq", None),
        P("doc", "seq", None),
    )
    return jax.shard_map(
        on_device, mesh=mesh, in_specs=in_specs, out_specs=out_specs, check_vma=False
    )
```

profile of v0, /device:TPU:0, one launch (start us, length us, event | category | flops | bytes accessed | tf_op | source)
XLA Modules:
  0.0 259.3 jit_solution(13848333703797358037)
XLA Ops:
  0.6 0.0 copy-start
  0.7 0.6 copy-done
  1.3 0.6 constant_dynamic-slice_fusion.2
  1.9 1.3 broadcast_in_dim.31
  3.2 1.3 broadcast_in_dim.32
  4.4 53.4 %go_forward.1 = (bf16[512,1024]{1,0:T(8,128)(2,1)}, bf16[2,4,512,128]{3,2,1,0:T(8,128)(2,1)}, bf16[2,4,512,128]{3,2,1,0:T(8,128)(2,1)}, bf16[2,4,512,128]{3,2,1,...) custom-call(s32[1]{0:T(128)} %bitcast.limit_ref, ...), custom_call_target="tpu_custom_call" | custom-call | tf_op jit(solution)/shard_map/go_forward/pallas_call | solution.py:731
  57.8 194.1 %go_back.1 = (bf16[512,1024]{1,0:T(8,128)(2,1)}, bf16[512,1024]{1,0:T(8,128)(2,1)}, f32[32,2816]{1,0:T(8,128)}, f32[32,2816]{1,0:T(8,128)}, f32[32,1024]{1,0:T(8...) custom-call(s32[1]{0:T(128)} %bitcast.limit_ref, ...), custom_call_target="tpu_custom_call" | custom-call | tf_op jit(solution)/shard_map/go_back/pallas_call | solution.py:1554
  251.9 0.7 reduce
  252.6 0.1 reshape.33
  252.7 0.5 fusion
  253.2 5.9 %deliver.1 = (bf16[512,1024]{1,0:T(8,128)(2,1)}, bf16[512,1024]{1,0:T(8,128)(2,1)}, f32[32,2816]{1,0:T(8,128)}, f32[32,2816]{1,0:T(8,128)}, f32[32,1024]{1,0:T(8...) custom-call(bf16[512,1024]{1,0:T(8,128)(2,1)} %get-tuple-element.56., ...), custom_call_target="tpu_custom_call" | custom-call | tf_op jit(solution)/shard_map/deliver/pallas_call | solution.py:1618
Async XLA Ops:
  0.6 0.7 copy-start
where the time goes:
time: 260 us; the launch traced here: 259 us
  Pallas kernels  253 us (97%)
  other arithmetic  3.28 us (1%)
    pallas_call x1, Pallas kernels, go_back(): pl.pallas_call(back_kernel, out_shape=(struct((block, width), low), struc...  194 us
    pallas_call x1, Pallas kernels, go_forward(): pl.pallas_call(front_kernel, out_shape=(struct((block, width), low), stru...  53.4 us
    pallas_call x1, Pallas kernels, deliver(): pl.pallas_call(deliver_kernel, out_shape=tuple((struct(a.shape, a.dtype)...  5.9 us

commit v1 on v0

--- a/solution.py
+++ b/solution.py
@@ -477,7 +477,7 @@
     seq_count, capacity = mem_in.shape[0], mem_in.shape[3]
     block, width = tokens.shape
     mem_rows, topk = tables.shape[1], every.shape[2]
-    limit = limit_ref[0]
+    limit = limit_ref[0, seq // BPS]
 
     loads = [
         pltpu.make_async_copy(src, dst, load_sem.at[i])
@@ -520,7 +520,7 @@
         at = pl.ds(pl.multiple_of(i * part, part), part)
         x = rows[at, :].astype(jnp.float32)
         factor = lax.rsqrt(jnp.mean(x * x, axis=-1, keepdims=True) + EPS)
-        normed[at, :] = (x * factor * gain[...]).astype(jnp.bfloat16)
+        normed[at, :] = (x * factor * gain[0:1, :]).astype(jnp.bfloat16)
         return carry
 
     lax.fori_loop(0, block // part, norm, 0)
@@ -755,65 +755,65 @@
 
 
 ALONG = (("x", "y", "low", "high"), ("y", "x", "low", "high"), ("low", "high", "y", "x"), ("low", "high", "x", "y"))
-TURNS = (1, 1, 3, 3, 1, 1, 2, 3, 0, 1, 0, 1, 1, 3, 3, 0, 1, 0, 0, 1, 2, 1, 2, 2, 2, 2, 3, 1, 1, 3, 1, 1, 3, 0, 1, 1, 0, 2, 2, 1, 1, 2)
+TURNS = (2, 0, 0, 3, 0, 1, 1, 1, 2, 1, 0, 0, 0, 0, 3, 0, 1, 0, 2, 0, 1, 3, 0, 0, 1, 1, 3, 1, 3, 0, 3, 1, 0, 0, 1, 0, 2, 0, 1, 2, 2, 3)
 PLAN = (
     (),
     ((0, 0), (1, 0),),
     ((2, 0), (3, 0),),
-    ((0, 1), (4, 0), (5, 0),),
-    ((1, 1), (2, 1), (6, 0), (7, 0), (0, 2),),
-    ((3, 1), (4, 1), (8, 0), (9, 0), (1, 2),),
-    ((5, 1), (10, 0), (11, 0), (6, 1), (2, 2), (4, 2),),
-    ((9, 1), (12, 0), (7, 1), (13, 0), (8, 1), (0, 3), (5, 2),),
-    ((11, 1), (1, 3), (14, 0), (15, 0), (10, 1), (4, 3), (3, 2), (2, 3),),
-    ((12, 1), (16, 0), (9, 2), (17, 0), (8, 2), (6, 2), (11, 2), (10, 2), (2, 4), (13, 1),),
-    ((18, 0), (5, 3), (19, 0), (7, 2), (15, 1), (0, 4), (3, 3), (1, 4), (16, 1), (12, 2), (14, 1),),
-    ((6, 3), (20, 0), (9, 3), (21, 0),),
-    ((8, 3), (4, 4), (11, 3), (17, 1), (10, 3), (19, 1),),
-    ((15, 2), (3, 4), (18, 1), (12, 3),),
-    ((7, 3), (16, 2), (13, 2), (6, 4), (21, 1), (5, 4),),
+    ((4, 0), (0, 1), (1, 1), (5, 0),),
+    ((6, 0), (2, 1), (3, 1), (7, 0), (1, 2),),
+    ((8, 0), (4, 1), (9, 0), (5, 1), (0, 2),),
+    ((1, 3), (10, 0), (11, 0), (6, 1), (3, 2), (5, 2),),
+    ((2, 2), (8, 1), (12, 0), (13, 0), (5, 3), (7, 1),),
+    ((1, 4), (10, 1), (14, 0), (4, 2), (15, 0), (2, 3),),
+    ((11, 1), (9, 1), (16, 0), (0, 3), (17, 0), (6, 2), (3, 3), (10, 2), (8, 2),),
+    ((5, 4), (18, 0), (14, 1), (19, 0), (4, 3), (12, 1), (11, 2), (6, 3), (10, 3),),
+    ((2, 4), (20, 0), (13, 1), (21, 0),),
+    ((16, 1), (3, 4), (7, 2), (8, 3),),
+    ((18, 1), (12, 2),),
+    ((15, 1),),
+    ((11, 3), (9, 2),),
+    ((20, 1), (0, 4),),
+    ((22, 0),),
+    ((23, 0), (14, 2), (13, 2), (24, 0), (4, 4),),
+    ((25, 0), (6, 4), (15, 2), (17, 1), (21, 1), (10, 4), (7, 3),),
     (),
-    ((19, 2), (17, 2), (22, 0), (20, 1),),
     (),
-    ((23, 0), (18, 2), (14, 2), (7, 4), (24, 0), (15, 3), (9, 4), (25, 0),),
-    ((8, 4), (16, 3), (11, 4), (19, 3),),
-    ((10, 4), (17, 3), (12, 4),),
-    ((13, 3),),
+    ((19, 1), (12, 3),),
+    ((9, 3), (24, 1), (38, 0), (16, 2), (8, 4), (13, 3),),
+    ((18, 2), (15, 3), (39, 0), (11, 4),),
+    ((25, 1),),
+    ((40, 0), (17, 2), (16, 3), (19, 2), (21, 2), (7, 4), (12, 4), (9, 4),),
+    ((13, 4), (15, 4), (41, 0),),
     (),
-    ((22, 1), (21, 2), (38, 0), (14, 3), (13, 4),),
+    ((39, 1), (20, 2), (38, 1),),
+    ((18, 3),),
+    ((22, 1),),
     (),
-    ((39, 0), (14, 4),),
-    ((23, 1), (20, 2), (18, 3), (40, 0), (24, 1),),
-    (),
-    ((41, 0), (15, 4), (25, 1),),
-    (),
-    ((39, 1), (16, 4), (20, 3), (19, 4), (21, 3), (17, 4),),
-    (),
-    ((22, 2),),
-    (),
-    ((40, 1), (39, 2), (38, 1), (20, 4),),
-    (),
-    ((23, 2),),
-    ((18, 4), (22, 3),),
-    ((23, 3), (24, 2),),
-    ((41, 1), (24, 3),),
-    (),
-    ((39, 3),),
-    ((25, 2), (21, 4), (40, 2),),
-    (),
-    ((25, 3),),
-    ((26, 0), (27, 0),),
-    ((28, 0), (29, 0),),
-    ((30, 0), (31, 0), (38, 2), (32, 0),),
-    ((40, 3), (33, 0), (34, 0), (27, 1), (35, 0), (22, 4),),
-    ((36, 0), (26, 1), (37, 0),),
-    ((28, 1), (23, 4),),
-    ((29, 1), (41, 2), (30, 1),),
-    ((24, 4), (25, 4), (32, 1), (39, 4),),
-    ((31, 1), (33, 1), (38, 3),),
-    ((40, 4), (27, 2), (37, 1),),
-    ((34, 1), (26, 2), (36, 1),),
-    ((28, 2), (27, 3), (35, 1), (30, 2), (29, 2), (41, 3), (28, 3), (31, 2), (38, 4), (33, 2), (30, 3), (32, 2), (34, 2), (36, 2), (31, 3), (26, 3), (33, 3), (37, 2), (35, 2), (34, 3), (27, 4), (29, 3), (26, 4), (36, 3), (28, 4), (41, 4), (30, 4), (37, 3), (32, 3), (35, 3), (29, 4), (31, 4), (33, 4), (37, 4), (32, 4), (34, 4), (36, 4), (35, 4),),
+    ((23, 1),),
+    ((14, 3), (22, 2), (40, 1),),
+    ((17, 3), (19, 3),),
+    ((16, 4),),
+    ((23, 2), (14, 4),),
+    ((41, 1), (24, 2),),
+    ((25, 2),),
+    ((21, 3), (20, 3), (22, 3), (38, 2), (18, 4), (39, 2), (23, 3), (24, 3), (25, 3), (40, 2), (17, 4), (19, 4),),
+    ((21, 4),),
+    ((39, 3), (38, 3),),
+    ((41, 2), (40, 3),),
+    ((20, 4), (22, 4), (26, 0), (39, 4), (27, 0), (23, 4),),
+    ((24, 4), (28, 0), (29, 0), (25, 4),),
+    ((41, 3), (30, 0), (40, 4), (31, 0), (38, 4),),
+    ((32, 0), (26, 1), (33, 0), (27, 1),),
+    ((41, 4), (34, 0), (29, 1),),
+    ((35, 0), (28, 1), (36, 0), (37, 0),),
+    ((31, 1), (32, 1),),
+    ((30, 1),),
+    ((34, 1), (33, 1),),
+    ((29, 2), (27, 2), (32, 2), (26, 2),),
+    ((36, 1), (33, 2), (35, 1),),
+    ((28, 2), (29, 3), (27, 3),),
+    ((32, 3), (37, 1), (35, 2), (30, 2), (31, 2), (33, 3), (34, 2), (37, 2), (26, 3), (35, 3), (28, 3), (36, 2), (31, 3), (30, 3), (29, 4), (34, 3), (27, 4), (26, 4), (37, 3), (32, 4), (28, 4), (33, 4), (36, 3), (30, 4), (35, 4), (31, 4), (36, 4), (34, 4), (37, 4),),
 )
 OFFERED = (20, 22, 24, 26)
 RING = 8
@@ -935,10 +935,10 @@
 
 def back_kernel(
     limit_ref, mixed_in, qb_in, kb_in, vb_in, qx_in, mkb_in, mvb_in, ob_in, lse_in0, spots_in,
-    tokens, cotangent, w_query, w_key, w_value, w_out, w_gate, w_up, w_down, gain, gain_two,
+    tokens, cotangent, w_query, w_key, w_value, w_out, w_gate, w_up, w_down, gains_in,
     layer_out, grad_tokens, gate_rows, up_rows, query_rows, key_rows, value_rows, out_rows, down_rows, gains_out,
-    mem_home, down, grad, middle_kept, grad_middle,
-    gb, gx, lse, delta, lse_in, delta_in, dq_cross, dqkv, mem_in, gain_buf, made, own, *rest,
+    mem_home, down, grad_middle,
+    gb, gx, lse, delta, lse_in, delta_in, dq_cross, dqkv, mem_in, gain_buf, made, own, grad, *rest,
 ):
     stages = [rest[5 * c : 5 * c + 5] for c in range(2)]
     sums = rest[10:12]
@@ -950,8 +950,8 @@
     core, chip, mate, across, diagonal = seats()
     seq, doc = lax.axis_index("seq"), lax.axis_index("doc")
     seq_count = mem_in.shape[0]
-    block = grad.shape[0]
-    limit = limit_ref[0]
+    block = tokens.shape[0]
+    limit = limit_ref[0, seq // BPS]
     peers = {
         "core": mate,
         "x": across,
@@ -1004,7 +1004,7 @@
             grad_copy(head, True).start()
             grad_copy(head, False).start()
 
-    def front(normed, normed_t, grad_y, total, back, hidden_t, mixed):
+    def front(normed, normed_t, grad_y, total, back, hidden_t, mixed, middle, w_in, w_back):
         width = total.shape[1]
         tiles = w_gate.shape[1] // UNIT
         part = 128
@@ -1021,7 +1021,7 @@
         def chunk(i):
             return pl.ds(pl.multiple_of(i * part, part), part)
 
-        def opening(rows, weights, middle):
+        def opening(rows, weights):
             loads = [
                 pltpu.make_async_copy(tokens, rows, front_sem.at[2]),
                 pltpu.make_async_copy(w_out, weights, front_sem.at[3]),
@@ -1036,13 +1036,11 @@
                 return carry
 
             lax.fori_loop(0, width // UNIT, join, 0)
-            keep = pltpu.make_async_copy(middle, middle_kept, front_sem.at[4])
-            keep.start()
 
             def norm(i, carry):
                 x = middle[chunk(i), :]
                 factor = lax.rsqrt(jnp.mean(x * x, axis=-1, keepdims=True) + EPS)
-                value = x * factor * gain_two[...]
+                value = x * factor * gains_in[1:2, :]
                 normed[chunk(i), :] = value.astype(jnp.bfloat16)
                 normed_t[:, chunk(i)] = value.T.astype(jnp.bfloat16)
                 total[chunk(i), :] = jnp.zeros((part, width), jnp.float32)
@@ -1050,34 +1048,32 @@
                 return carry
 
             lax.fori_loop(0, block // part, norm, 0)
-            keep.wait()
-
+
+        def tile_loads(tile):
+            slot = tile % 2
+            return (
+                pltpu.make_async_copy(w_gate.at[:, strip(tile)], w_in.at[slot, 0], tile_sem.at[slot, 0]),
+                pltpu.make_async_copy(w_up.at[:, strip(tile)], w_in.at[slot, 1], tile_sem.at[slot, 1]),
+                pltpu.make_async_copy(w_down.at[strip(tile), :], w_back.at[slot], tile_sem.at[slot, 2]),
+            )
+
+        for copy in tile_loads(0):
+            copy.start()
         pl.run_scoped(
             opening,
-            pltpu.VMEM(tokens.shape, jnp.bfloat16), pltpu.VMEM(w_out.shape, jnp.bfloat16), pltpu.VMEM(total.shape, jnp.float32),
-        )
-
-        def hidden_units(w_in, w_back):
-            def loads(tile):
-                slot = tile % 2
-                return (
-                    pltpu.make_async_copy(w_gate.at[:, strip(tile)], w_in.at[slot, 0], tile_sem.at[slot, 0]),
-                    pltpu.make_async_copy(w_up.at[:, strip(tile)], w_in.at[slot, 1], tile_sem.at[slot, 1]),
-                    pltpu.make_async_copy(w_down.at[strip(tile), :], w_back.at[slot], tile_sem.at[slot, 2]),
-                )
-
-            for copy in loads(0):
-                copy.start()
-
+            pltpu.VMEM(tokens.shape, jnp.bfloat16), pltpu.VMEM(w_out.shape, jnp.bfloat16),
+        )
+
+        def hidden_units():
             def one(tile, carry):
                 slot = tile % 2
 
                 @pl.when(tile + 1 < tiles)
                 def _():
-                    for copy in loads(tile + 1):
+                    for copy in tile_loads(tile + 1):
                         copy.start()
 
-                for copy in loads(tile):
+                for copy in tile_loads(tile):
                     copy.wait()
                 opened = matmul(normed[...], w_in[slot, 0], NN)
                 upper = matmul(normed[...], w_in[slot, 1], NN)
@@ -1097,21 +1093,16 @@
 
             lax.fori_loop(0, tiles, one, 0)
 
-        pl.run_scoped(
-            hidden_units,
-            pltpu.VMEM((2, 2, width, UNIT), jnp.bfloat16), pltpu.VMEM((2, UNIT, width), jnp.bfloat16),
-        )
-
-        def closing(middle, weights, branch, branch_back, stage_down):
+        hidden_units()
+
+        def closing(branch, stage_down):
             loads = [
-                pltpu.make_async_copy(middle_kept, middle, front_sem.at[2]),
-                pltpu.make_async_copy(w_out, weights, front_sem.at[3]),
+                pltpu.make_async_copy(w_out.at[:, strip(p)], w_in.at[p // 2, p % 2], tile_sem.at[p // 2, p % 2])
+                for p in range(4)
             ]
             for copy in loads:
                 copy.start()
             engine.run(11)
-            for copy in loads:
-                copy.wait()
 
             def norm_back(i, carry):
                 x = middle[chunk(i), :]
@@ -1119,7 +1110,7 @@
                 unit = x * factor
                 grad_normed = back[chunk(i), :]
                 normed[chunk(i), :] = (x + total[chunk(i), :]).astype(jnp.bfloat16)
-                scaled = gain_two[...] * grad_normed
+                scaled = gains_in[1:2, :] * grad_normed
                 inner = jnp.mean(scaled * unit, axis=-1, keepdims=True)
                 value = grad_y[chunk(i), :].astype(jnp.float32) + factor * (scaled - unit * inner)
                 middle[chunk(i), :] = value
@@ -1136,16 +1127,18 @@
 
             engine.run(12)
 
-            def to_attended(j, carry):
-                branch_back[:, strip(j)] = matmul(branch[...], weights[strip(j), :], NT).astype(jnp.bfloat16)
-                return carry
-
-            lax.fori_loop(0, width // UNIT, to_attended, 0)
-            store = pltpu.make_async_copy(branch_back, grad, front_sem.at[1])
-            store.start()
+            for copy in loads:
+                copy.wait()
+            for j in (0, 2, 1, 3):
+                at = slice(j * UNIT, (j + 1) * UNIT)
+                value = 0.0
+                for p in range(4):
+                    value = value + matmul(branch[:, p * UNIT : (p + 1) * UNIT], w_in[p // 2, p % 2, at, :], NT)
+                grad[:, at] = value.astype(jnp.bfloat16)
+                if j == 2:
+                    far_start(0)
             engine.run(13)
-            store.wait()
-            far_start(0)
+            far_start(1)
             share_heads((grad,), (gb,), core, mate, gb_local, gb_send, gb_recv)
 
             def turn_over(i, carry):
@@ -1179,8 +1172,8 @@
                 down_part(2 * m + 1)
                 for j in range(3):
                     pl.when(m == 2 * j + 2)(lambda: engine.offer_down(j))
-                pl.when(m == 1)(lambda: far_start(1))
-                pl.when(m == 4)(lambda: far_start(2))
+                pl.when(m == 1)(lambda: far_start(2))
+                pl.when(m == 4)(lambda: far_start(3))
                 engine.run_turn(18, m, 8)
                 return carry
 
@@ -1188,14 +1181,12 @@
             down_store(14).wait()
             down_store(15).wait()
             engine.offer_down(3)
-            far_start(3)
             for copy in writes:
                 copy.wait()
 
         pl.run_scoped(
             closing,
-            pltpu.VMEM(total.shape, jnp.float32), pltpu.VMEM(w_out.shape, jnp.bfloat16),
-            pltpu.VMEM(normed.shape, jnp.bfloat16), pltpu.VMEM(normed.shape, jnp.bfloat16),
+            pltpu.VMEM(normed.shape, jnp.bfloat16),
             pltpu.VMEM((2, 2, 2, 2, ROWS[1], UNIT), jnp.bfloat16),
         )
 
@@ -1204,6 +1195,8 @@
         pltpu.VMEM(tokens.shape, jnp.bfloat16), pltpu.VMEM((tokens.shape[1], block), jnp.bfloat16),
         pltpu.VMEM(tokens.shape, jnp.bfloat16), pltpu.VMEM(tokens.shape, jnp.float32), pltpu.VMEM(tokens.shape, jnp.float32),
         pltpu.VMEM((w_gate.shape[1], block), jnp.bfloat16), pltpu.VMEM(tokens.shape, jnp.bfloat16),
+        pltpu.VMEM(tokens.shape, jnp.float32), pltpu.VMEM((2, 2, tokens.shape[1], UNIT), jnp.bfloat16),
+        pltpu.VMEM((2, UNIT, tokens.shape[1]), jnp.bfloat16),
     )
 
     def attention(qb, kb, vb, qx, mkb, mvb, ob, dq_own, dk_sum, dv_sum, dm, dqkv_mate, mem_out, spots):
@@ -1385,7 +1378,7 @@
             at = pl.ds(pl.multiple_of(i * 2 * part, 2 * part), 2 * part)
             x = rows[at, :].astype(jnp.float32)
             factor = lax.rsqrt(jnp.mean(x * x, axis=-1, keepdims=True) + EPS)
-            normed[:, at] = (x * factor * gain[...]).T.astype(jnp.bfloat16)
+            normed[:, at] = (x * factor * gains_in[0:1, :]).T.astype(jnp.bfloat16)
             return carry
 
         lax.fori_loop(0, block // (2 * part), norm, 0)
@@ -1431,7 +1424,7 @@
             factor = lax.rsqrt(jnp.mean(x * x, axis=-1, keepdims=True) + EPS)
             unit = x * factor
             grad_normed = dx[at, :]
-            scaled = gain[...] * grad_normed
+            scaled = gains_in[0:1, :] * grad_normed
             inner = jnp.mean(scaled * unit, axis=-1, keepdims=True)
             rows[at, :] = (middle[at, :] + factor * (scaled - unit * inner)).astype(jnp.bfloat16)
             return carry + jnp.sum(grad_normed * unit, axis=0, keepdims=True)
@@ -1509,7 +1502,7 @@
             grad_copy(head, False).wait_send()
 
 
-def go_back(limit, attended, saved, tokens, cotangent, weights, gain, gain_two):
+def go_back(limit, attended, saved, tokens, cotangent, weights, gains):
     block, width = tokens.shape
     low, full = jnp.bfloat16, jnp.float32
     box = (2, HALF, block, HEAD_DIM)
@@ -1536,6 +1529,7 @@
         pltpu.VMEM((2, 5, 2, 1, width), full),
         pltpu.VMEM((RING, 2, 2, 2, 2, 2, ROWS[0], UNIT), low),
         pltpu.VMEM((2, 2, 2, 2, 2, ROWS[1], UNIT), low),
+        pltpu.VMEM((block, width), low),
     ]
     for c in range(2):
         scratch += [pltpu.VMEM((units[c],) + (2,) * k + (ROWS[c], UNIT), low) for k in (4, 3, 2, 1, 0)]
@@ -1560,14 +1554,14 @@
             struct((88, width), full), struct((2, 1, width), full),
             struct(mem, low),
             wide(88, width),
-            struct((block, width), low), struct((block, width), full), struct((block, width), full),
+            struct((block, width), full),
         ),
-        in_specs=[pl.BlockSpec(memory_space=pltpu.SMEM)] + [hbm] * 19 + [vmem] * 2,
-        out_specs=(hbm,) * 9 + (vmem,) + (hbm,) * 5,
+        in_specs=[pl.BlockSpec(memory_space=pltpu.SMEM)] + [hbm] * 19 + [vmem],
+        out_specs=(hbm,) * 9 + (vmem,) + (hbm,) * 3,
         scratch_shapes=scratch,
         name="go_back",
         compiler_params=pltpu.CompilerParams(collective_id=3, has_side_effects=True, vmem_limit_bytes=60 * 2**20),
-    )(limit, attended, *saved, tokens, cotangent, *weights, gain, gain_two)
+    )(limit, attended, *saved, tokens, cotangent, *weights, gains)
     return deliver(results[:9], results[10], picked_t) + (results[9],)
 
 
@@ -1679,21 +1673,21 @@
     gain_one = attn_gain.astype(jnp.float32)
     gain_two = ffn_gain.astype(jnp.float32)
     if fitting():
+        gains = jnp.stack((attn_gain, ffn_gain)).astype(jnp.float32)
         attended, *saved = go_forward(
-            limit, tokens[0], gain_one[None], (w_query, w_key, w_value), mem_keys[0], mem_values[0], mem_idx[0]
-        )
-        layer_out, grad_tokens, gate_rows, up_rows, query_rows, key_rows, value_rows, out_rows, down_rows, grad_mk, grad_mv, gains = go_back(
-            limit,
+            seg_len, tokens[0], gains, (w_query, w_key, w_value), mem_keys[0], mem_values[0], mem_idx[0]
+        )
+        layer_out, grad_tokens, gate_rows, up_rows, query_rows, key_rows, value_rows, out_rows, down_rows, grad_mk, grad_mv, summed = go_back(
+            seg_len,
             attended,
             saved,
             tokens[0],
             cotangent[0],
             (w_query, w_key, w_value, w_out, w_gate, w_up, w_down),
-            gain_one[None],
-            gain_two[None],
+            gains,
         )
         index = lax.axis_index("seq") * lax.axis_size("doc") + lax.axis_index("doc")
-        parts = gains.reshape(2, seq_count * lax.axis_size("doc"), -1)
+        parts = summed.reshape(2, seq_count * lax.axis_size("doc"), -1)
         attn_row, ffn_row = lax.dynamic_index_in_dim(parts, index, 1, keepdims=False)
         return (
             layer_out[None],

time: 260 us -> 243 us (0.935)
  Pallas kernels: 253 us -> 239 us
  other arithmetic: 3.28 us -> 0.64 us
    pallas_call x1, Pallas kernels: 194 us -> 180 us  [go_back(): pl.pallas_call(back_kernel, out_shape=(struct((block, width), low), struc...]
where the time goes in v1:
time: 243 us; the launch traced here: 242 us
  Pallas kernels  239 us (98%)
    pallas_call x1, Pallas kernels, go_back(): pl.pallas_call(back_kernel, out_shape=(struct((block, width), low), struc...  180 us
    pallas_call x1, Pallas kernels, go_forward(): pl.pallas_call(front_kernel, out_shape=(struct((block, width), low), stru...  52.8 us
    pallas_call x1, Pallas kernels, deliver(): pl.pallas_call(deliver_kernel, out_shape=tuple((struct(a.shape, a.dtype)...  5.91 us

profile of v1, /device:TPU:0, one launch (start us, length us, event | category | flops | bytes accessed | tf_op | source)
XLA Modules:
  0.0 242.3 jit_solution(7186164440467781900)
XLA Ops:
  0.6 0.7 stack.10
  1.3 0.7 stack.9
  2.0 0.6 maximum_convert_fusion.gain.gains_in
  2.6 52.8 %go_forward.1 = (bf16[512,1024]{1,0:T(8,128)(2,1)}, bf16[2,4,512,128]{3,2,1,0:T(8,128)(2,1)}, bf16[2,4,512,128]{3,2,1,0:T(8,128)(2,1)}, bf16[2,4,512,128]{3,2,1,...) custom-call(s32[1,2]{1,0:T(1,128)} %limit_ref.3, ...), custom_call_target="tpu_custom_call" | custom-call | tf_op jit(solution)/shard_map/go_forward/pallas_call | solution.py:731
  55.4 180.3 %go_back.1 = (bf16[512,1024]{1,0:T(8,128)(2,1)}, bf16[512,1024]{1,0:T(8,128)(2,1)}, f32[32,2816]{1,0:T(8,128)}, f32[32,2816]{1,0:T(8,128)}, f32[32,1024]{1,0:T(8...) custom-call(s32[1,2]{1,0:T(1,128)} %limit_ref.3, ...), custom_call_target="tpu_custom_call" | custom-call | tf_op jit(solution)/shard_map/go_back/pallas_call | solution.py:1548
  235.7 0.0 copy-start
  235.7 5.9 %deliver.1 = (bf16[512,1024]{1,0:T(8,128)(2,1)}, bf16[512,1024]{1,0:T(8,128)(2,1)}, f32[32,2816]{1,0:T(8,128)}, f32[32,2816]{1,0:T(8,128)}, f32[32,1024]{1,0:T(8...) custom-call(bf16[512,1024]{1,0:T(8,128)(2,1)} %get-tuple-element.56., ...), custom_call_target="tpu_custom_call" | custom-call | tf_op jit(solution)/shard_map/deliver/pallas_call | solution.py:1612
  241.6 0.0 copy-done
  241.7 0.1 reshape.33
  241.8 0.5 dynamic-slice_bitcast_fusion
  (1 shorter events, 0.0 us)
Async XLA Ops:
  235.7 5.9 %copy-start = (f32[2,1,1024]{2,1,0:T(1,128)S(1)}, f32[2,1,1024]{2,1,0:T(1,128)}, u32[]{:S(2)}) copy-start(f32[2,1,1024]{2,1,0:T(1,128)} %get-tuple-element.69) | copy-start | bytes 24580

commit v2 on v1

--- a/solution.py
+++ b/solution.py
@@ -464,12 +464,17 @@
     return (before < lax.broadcasted_iota(jnp.int32, (rank_of, rank_of), 1)).astype(jnp.bfloat16)
 
 
+def one_row(ref):
+    value = ref[...].astype(jnp.float32)
+    return jnp.concatenate([value[i : i + 1] for i in range(value.shape[0])], axis=1)
+
+
 def front_kernel(
-    limit_ref, tokens, gain, w_query, w_key, w_value, mem_keys, mem_values, wanted,
+    limit_ref, tokens, gain_in, w_query, w_key, w_value, mem_keys, mem_values, wanted,
     attended, qb, kb, vb, qx, mkb, mvb, ob, lse, spots, pick_t,
     rows, weights, normed, qkv, tables, every, pick, mem_out, mem_in,
     mixed_own, mixed_out, mixed_in, lse_out, lse_in,
-    load_sem, want_send, want_recv, mem_send, mem_recv, mem_local,
+    gain, load_sem, want_send, want_recv, mem_send, mem_recv, mem_local,
     local_sem, mate_send, mate_recv, far_send, far_recv, back_send, back_recv, end_sem,
 ):
     core, chip, mate, across, diagonal = seats()
@@ -513,6 +518,7 @@
 
     for away in range(1, seq_count):
         want_copy(away).start()
+    gain[...] = one_row(gain_in)
     loads[1].wait()
     part = 64
 
@@ -534,8 +540,6 @@
             return carry
 
         lax.fori_loop(0, width // UNIT, one, 0)
-
-    project(0)
 
     def query_copy(head, own):
         return remote(
@@ -551,11 +555,17 @@
             qkv.at[0, :, head_lanes(core, head)], qx.at[far, head], far_send.at[0, head], far_recv.at[far, head], across
         )
 
-    @pl.when(chip == 1)
-    def _():
-        for head in range(HALF):
-            query_copy(head, True).start()
-            query_copy(head, False).start()
+    loads[2].wait()
+    for pair in range(HALF // 2):
+        for side in range(2):
+            lanes = slice((side * HALF // 2 + pair) * UNIT, (side * HALF // 2 + pair + 1) * UNIT)
+            qkv[0, :, lanes] = matmul(normed[...], weights[0, :, lanes], NN).astype(jnp.bfloat16)
+
+        @pl.when(chip == 1)
+        def _():
+            for head in (2 * pair, 2 * pair + 1):
+                query_copy(head, True).start()
+                query_copy(head, False).start()
 
     project(1)
     project(2)
@@ -745,6 +755,7 @@
             pltpu.VMEM(mem, low), pltpu.VMEM(mem, low),
             pltpu.VMEM(flat, full), pltpu.VMEM(flat, low), pltpu.VMEM(flat, low),
             pltpu.VMEM(row, full), pltpu.VMEM(row, full),
+            pltpu.VMEM((1, width), full),
             dma((7,)), dma((seq_count - 1,)), dma((seq_count - 1,)), dma((seq_count - 1,)), dma((seq_count - 1,)), dma((1,)),
             dma((3, HALF)), dma((3, HALF)), dma((3, HALF)),
             dma((2, HALF)), dma((2, HALF)), dma((2, 2, HALF)), dma((2, 2, HALF)), dma((3, HALF)),
@@ -826,10 +837,10 @@
 
 
 class Sums:
-    def __init__(self, down, made, own, stages, sums, local_sem, send_sem, recv_sem, peers):
+    def __init__(self, down, made, own, stages, sums, homes, local_sem, send_sem, recv_sem, done_sem, peers):
         self.down, self.made, self.own, self.stages, self.sums = down, made, own, stages, sums
         self.local_sem, self.send_sem, self.recv_sem = local_sem, send_sem, recv_sem
-        self.peers = peers
+        self.peers, self.homes, self.done_sem = peers, homes, done_sem
         seq, doc = lax.axis_index("seq"), lax.axis_index("doc")
         self.bits = {
             "core": seq % 2,
@@ -910,8 +921,24 @@
                 ref[index] = ref[index] + kept
             else:
                 self.sums[kind][index] = ref[index].astype(jnp.float32) + kept.astype(jnp.float32)
+                self.result(unit).start()
         if level < 4:
             self.copy(kind, index, order, level + 1).start()
+
+    def result(self, unit):
+        gate, up, out, query, key, value, down = self.homes
+        if unit < 22:
+            home, place = (gate, up)[unit % 2], unit // 2
+        elif unit < 26:
+            home, place = out, unit - 22
+        elif unit < NARROW:
+            home, place = (query, key, value)[(unit - 26) // 4], (unit - 26) % 4
+        else:
+            home, place = down, unit - NARROW
+        kind = 0 if unit < NARROW else 1
+        return pltpu.make_async_copy(
+            self.sums[kind].at[unit - kind * NARROW], home.at[:, pl.ds(place * UNIT, UNIT)], self.done_sem.at[unit]
+        )
 
     def run(self, place):
         for unit, level in PLAN[place]:
@@ -922,23 +949,22 @@
             if PLAN[first + k]:
                 pl.when(turn == k)(lambda: self.run(first + k))
 
-    def drain(self):
-        for kind, count in enumerate((NARROW, 4)):
-            def one(index, carry):
-                pl.when((kind == 1) | (index >= NARROW - RING))(lambda: self.core_copy(kind, index).wait_send())
-                for level in range(1, 5):
-                    self.copy(kind, index, ALONG[0], level).wait_send()
-                return carry
-
-            lax.fori_loop(0, count, one, 0)
+    def drain(self, kind, first, last):
+        def one(index, carry):
+            pl.when((kind == 1) | (index >= NARROW - RING))(lambda: self.core_copy(kind, index).wait_send())
+            for level in range(1, 5):
+                self.copy(kind, index, ALONG[0], level).wait_send()
+            return carry
+
+        lax.fori_loop(first, last, one, 0)
 
 
 def back_kernel(
     limit_ref, mixed_in, qb_in, kb_in, vb_in, qx_in, mkb_in, mvb_in, ob_in, lse_in0, spots_in,
-    tokens, cotangent, w_query, w_key, w_value, w_out, w_gate, w_up, w_down, gains_in,
+    tokens, cotangent, w_query, w_key, w_value, w_out, w_gate, w_up, w_down, gain_one_in, gain_two_in,
     layer_out, grad_tokens, gate_rows, up_rows, query_rows, key_rows, value_rows, out_rows, down_rows, gains_out,
     mem_home, down, grad_middle,
-    gb, gx, lse, delta, lse_in, delta_in, dq_cross, dqkv, mem_in, gain_buf, made, own, grad, *rest,
+    gb, gx, lse, delta, lse_in, delta_in, dq_cross, dqkv, mem_in, gain_buf, made, own, grad, gains_in, *rest,
 ):
     stages = [rest[5 * c : 5 * c + 5] for c in range(2)]
     sums = rest[10:12]
@@ -960,8 +986,8 @@
         "high": (seq, flip(doc, 2)),
     }
     others = [(lax.rem(seq + away, seq_count), doc) for away in range(1, seq_count)]
-    meet(others + [peers["low"], peers["high"]])
-    engine = Sums(down, made, own, stages, sums, local_sem, send_sems, recv_sems, peers)
+    homes = (gate_rows, up_rows, out_rows, query_rows, key_rows, value_rows, down_rows)
+    engine = Sums(down, made, own, stages, sums, homes, local_sem, send_sems, recv_sems, done_sem, peers)
 
     def grad_copy(head, own):
         return remote(
@@ -1028,6 +1054,9 @@
             ]
             for copy in loads:
                 copy.start()
+            meet(others + [peers["low"], peers["high"]])
+            gains_in[0:1, :] = one_row(gain_one_in)
+            gains_in[1:2, :] = one_row(gain_two_in)
             for copy in copies + loads:
                 copy.wait()
 
@@ -1283,6 +1312,33 @@
             for copy in row_copies():
                 copy.wait_recv()
 
+        def results(blk, head, which):
+            values = {}
+            if 0 in which:
+                values[0] = (dq_own[blk, head].T * SCALE).astype(jnp.bfloat16)
+            if 1 in which:
+                values[1] = (dk_sum[blk, head] * SCALE).astype(jnp.bfloat16)
+                values[2] = dv_sum[blk, head].astype(jnp.bfloat16)
+            return values
+
+        def hand_out(which):
+            def for_mate(head, carry):
+                for i, value in results(1 - core, head, which).items():
+                    dqkv_mate[i, head] = value
+                    mate_copy(dqkv_mate, i, head).start()
+                return carry
+
+            def for_own(head, carry):
+                for i, value in results(core, head, which).items():
+                    dqkv[i, :, head_lanes(core, head)] = value
+                return carry
+
+            lax.fori_loop(0, HALF, for_mate, 0)
+            lax.fori_loop(0, HALF, for_own, 0)
+
+        pl.when(chip == 0)(lambda: hand_out((0,)))
+        pl.when(chip == 1)(lambda: hand_out((1,)))
+
         def far_turn(i, carry):
             head, blk = i // 2, i % 2
 
@@ -1313,27 +1369,9 @@
 
         lax.fori_loop(0, 2 * HALF, far_turn, 0)
 
-        def results(blk, head):
-            return (
-                (dq_own[blk, head].T * SCALE).astype(jnp.bfloat16),
-                (dk_sum[blk, head] * SCALE).astype(jnp.bfloat16),
-                dv_sum[blk, head].astype(jnp.bfloat16),
-            )
-
-        def for_mate(head, carry):
-            for i, value in enumerate(results(1 - core, head)):
-                dqkv_mate[i, head] = value
-                mate_copy(dqkv_mate, i, head).start()
-            return carry
-
-        def for_own(head, carry):
-            for i, value in enumerate(results(core, head)):
-                dqkv[i, :, head_lanes(core, head)] = value
-            return carry
-
-        lax.fori_loop(0, HALF, for_mate, 0)
+        pl.when(chip == 0)(lambda: hand_out((1,)))
+        pl.when(chip == 1)(lambda: hand_out((0,)))
         engine.run(40)
-        lax.fori_loop(0, HALF, for_own, 0)
         engine.run(41)
         for away in range(1, seq_count):
             mem_copy(mem_out, away).wait_send()
@@ -1449,6 +1487,8 @@
         engine.run(54)
         engine.run(55)
         events = PLAN[56]
+        early = [n for n, (unit, level) in enumerate(events) if level == 3 and (unit < 26 or unit >= NARROW)]
+        emptied = max(early + [-1]) + 1
         stops = [len(events) * k // 6 for k in range(1, 6)]
         for n, (unit, level) in enumerate(events):
             for step in range(5):
@@ -1460,24 +1500,17 @@
                         gain_copy(step + 1).start()
                     else:
                         gains_out[...] = total
+            if n == emptied:
+                engine.drain(0, 0, 26)
+                engine.drain(1, 0, 4)
             engine.arrive(unit, level)
-        homes = []
-        for u in range(11):
-            homes += [(0, 2 * u, gate_rows, u), (0, 2 * u + 1, up_rows, u)]
-        for j in range(4):
-            homes += [(0, 22 + j, out_rows, j), (0, 26 + j, query_rows, j), (0, 30 + j, key_rows, j), (0, 34 + j, value_rows, j)]
-            homes.append((1, j, down_rows, j))
-        outs = []
-        for i, (kind, unit, ref, place) in enumerate(homes):
-            outs.append(
-                pltpu.make_async_copy(sums[kind].at[unit], ref.at[:, pl.ds(place * UNIT, UNIT)], done_sem.at[i])
-            )
-            outs[-1].start()
-        engine.drain()
+        engine.drain(0, 26, NARROW)
         for level in range(5):
             gain_copy(level).wait_send()
-        for copy in outs + [out_copy, mem_copy_out]:
+        for copy in [out_copy, mem_copy_out]:
             copy.wait()
+        for unit in range(NARROW + 4):
+            engine.result(unit).wait()
 
     width = w_query.shape[0]
     pl.run_scoped(
@@ -1502,7 +1535,7 @@
             grad_copy(head, False).wait_send()
 
 
-def go_back(limit, attended, saved, tokens, cotangent, weights, gains):
+def go_back(limit, attended, saved, tokens, cotangent, weights, gain_one, gain_two):
     block, width = tokens.shape
     low, full = jnp.bfloat16, jnp.float32
     box = (2, HALF, block, HEAD_DIM)
@@ -1530,6 +1563,7 @@
         pltpu.VMEM((RING, 2, 2, 2, 2, 2, ROWS[0], UNIT), low),
         pltpu.VMEM((2, 2, 2, 2, 2, ROWS[1], UNIT), low),
         pltpu.VMEM((block, width), low),
+        pltpu.VMEM((2, width), full),
     ]
     for c in range(2):
         scratch += [pltpu.VMEM((units[c],) + (2,) * k + (ROWS[c], UNIT), low) for k in (4, 3, 2, 1, 0)]
@@ -1556,12 +1590,12 @@
             wide(88, width),
             struct((block, width), full),
         ),
-        in_specs=[pl.BlockSpec(memory_space=pltpu.SMEM)] + [hbm] * 19 + [vmem],
+        in_specs=[pl.BlockSpec(memory_space=pltpu.SMEM)] + [hbm] * 19 + [vmem] * 2,
         out_specs=(hbm,) * 9 + (vmem,) + (hbm,) * 3,
         scratch_shapes=scratch,
         name="go_back",
         compiler_params=pltpu.CompilerParams(collective_id=3, has_side_effects=True, vmem_limit_bytes=60 * 2**20),
-    )(limit, attended, *saved, tokens, cotangent, *weights, gains)
+    )(limit, attended, *saved, tokens, cotangent, *weights, gain_one, gain_two)
     return deliver(results[:9], results[10], picked_t) + (results[9],)
 
 
@@ -1673,9 +1707,9 @@
     gain_one = attn_gain.astype(jnp.float32)
     gain_two = ffn_gain.astype(jnp.float32)
     if fitting():
-        gains = jnp.stack((attn_gain, ffn_gain)).astype(jnp.float32)
+        gain_rows = [gain.reshape(8, -1) for gain in (attn_gain, ffn_gain)]
         attended, *saved = go_forward(
-            seg_len, tokens[0], gains, (w_query, w_key, w_value), mem_keys[0], mem_values[0], mem_idx[0]
+            seg_len, tokens[0], gain_rows[0], (w_query, w_key, w_value), mem_keys[0], mem_values[0], mem_idx[0]
         )
         layer_out, grad_tokens, gate_rows, up_rows, query_rows, key_rows, value_rows, out_rows, down_rows, grad_mk, grad_mv, summed = go_back(
             seg_len,
@@ -1684,7 +1718,7 @@
             tokens[0],
             cotangent[0],
             (w_query, w_key, w_value, w_out, w_gate, w_up, w_down),
-            gains,
+            *gain_rows,
         )
         index = lax.axis_index("seq") * lax.axis_size("doc") + lax.axis_index("doc")
         parts = summed.reshape(2, seq_count * lax.axis_size("doc"), -1)

time: 243 us -> 238 us (0.979)
  Pallas kernels: 239 us -> 236 us
where the time goes in v2:
time: 238 us; the launch traced here: 237 us
  Pallas kernels  236 us (99%)
    pallas_call x1, Pallas kernels, go_back(): pl.pallas_call(back_kernel, out_shape=(struct((block, width), low), struc...  178 us
    pallas_call x1, Pallas kernels, go_forward(): pl.pallas_call(front_kernel, out_shape=(struct((block, width), low), stru...  51.7 us
    pallas_call x1, Pallas kernels, deliver(): pl.pallas_call(deliver_kernel, out_shape=tuple((struct(a.shape, a.dtype)...  5.91 us

profile of v2, /device:TPU:0, one launch (start us, length us, event | category | flops | bytes accessed | tf_op | source)
XLA Modules:
  0.0 237.4 jit_solution(16450275690259139215)
XLA Ops:
  0.6 51.7 %go_forward.1 = (bf16[512,1024]{1,0:T(8,128)(2,1)}, bf16[2,4,512,128]{3,2,1,0:T(8,128)(2,1)}, bf16[2,4,512,128]{3,2,1,0:T(8,128)(2,1)}, bf16[2,4,512,128]{3,2,1,...) custom-call(s32[1,2]{1,0:T(1,128)} %limit_ref.3, ...), custom_call_target="tpu_custom_call" | custom-call | tf_op jit(solution)/shard_map/go_forward/pallas_call | solution.py:741
  52.4 178.5 %go_back.1 = (bf16[512,1024]{1,0:T(8,128)(2,1)}, bf16[512,1024]{1,0:T(8,128)(2,1)}, f32[32,2816]{1,0:T(8,128)}, f32[32,2816]{1,0:T(8,128)}, f32[32,1024]{1,0:T(8...) custom-call(s32[1,2]{1,0:T(1,128)} %limit_ref.3, ...), custom_call_target="tpu_custom_call" | custom-call | tf_op jit(solution)/shard_map/go_back/pallas_call | solution.py:1582
  230.9 0.0 copy-start
  230.9 5.9 %deliver.1 = (bf16[512,1024]{1,0:T(8,128)(2,1)}, bf16[512,1024]{1,0:T(8,128)(2,1)}, f32[32,2816]{1,0:T(8,128)}, f32[32,2816]{1,0:T(8,128)}, f32[32,1024]{1,0:T(8...) custom-call(bf16[512,1024]{1,0:T(8,128)(2,1)} %get-tuple-element.56., ...), custom_call_target="tpu_custom_call" | custom-call | tf_op jit(solution)/shard_map/deliver/pallas_call | solution.py:1646
  236.8 0.0 copy-done
  236.8 0.1 reshape.41
  236.9 0.5 dynamic-slice_bitcast_fusion
  (1 shorter events, 0.0 us)
Async XLA Ops:
  230.9 5.9 %copy-start = (f32[2,1,1024]{2,1,0:T(1,128)S(1)}, f32[2,1,1024]{2,1,0:T(1,128)}, u32[]{:S(2)}) copy-start(f32[2,1,1024]{2,1,0:T(1,128)} %get-tuple-element.69) | copy-start | bytes 24580

commit v3 on v2

--- a/solution.py
+++ b/solution.py
@@ -1081,8 +1081,8 @@
         def tile_loads(tile):
             slot = tile % 2
             return (
-                pltpu.make_async_copy(w_gate.at[:, strip(tile)], w_in.at[slot, 0], tile_sem.at[slot, 0]),
-                pltpu.make_async_copy(w_up.at[:, strip(tile)], w_in.at[slot, 1], tile_sem.at[slot, 1]),
+                pltpu.make_async_copy(w_gate.at[:, strip(tile)], w_in.at[slot, :, 0:UNIT], tile_sem.at[slot, 0]),
+                pltpu.make_async_copy(w_up.at[:, strip(tile)], w_in.at[slot, :, UNIT : 2 * UNIT], tile_sem.at[slot, 1]),
                 pltpu.make_async_copy(w_down.at[strip(tile), :], w_back.at[slot], tile_sem.at[slot, 2]),
             )
 
@@ -1104,8 +1104,8 @@
 
                 for copy in tile_loads(tile):
                     copy.wait()
-                opened = matmul(normed[...], w_in[slot, 0], NN)
-                upper = matmul(normed[...], w_in[slot, 1], NN)
+                opened = matmul(normed[...], w_in[slot, :, 0:UNIT], NN)
+                upper = matmul(normed[...], w_in[slot, :, UNIT : 2 * UNIT], NN)
                 sigma = 1.0 / (1.0 + jnp.exp(-opened))
                 gated = opened * sigma
                 hidden = gated * upper
@@ -1114,7 +1114,7 @@
                 grad_hidden = matmul(grad_y[...], w_back[slot], NT)
                 grad_opened = (grad_hidden * upper * sigma * (1.0 + opened * (1.0 - sigma))).astype(jnp.bfloat16)
                 grad_upper = (grad_hidden * gated).astype(jnp.bfloat16)
-                back[...] += matmul(grad_opened, w_in[slot, 0], NT) + matmul(grad_upper, w_in[slot, 1], NT)
+                back[...] += matmul(jnp.concatenate((grad_opened, grad_upper), axis=1), w_in[slot], NT)
                 for kind, value in enumerate((grad_opened, grad_upper)):
                     engine.put(2 * tile + kind, matmul(normed_t[...], value, NN))
                 engine.run_turn(0, tile, tiles)
@@ -1126,7 +1126,7 @@
 
         def closing(branch, stage_down):
             loads = [
-                pltpu.make_async_copy(w_out.at[:, strip(p)], w_in.at[p // 2, p % 2], tile_sem.at[p // 2, p % 2])
+                pltpu.make_async_copy(w_out.at[:, strip(p)], w_in.at[p // 2, :, (p % 2) * UNIT : (p % 2 + 1) * UNIT], tile_sem.at[p // 2, p % 2])
                 for p in range(4)
             ]
             for copy in loads:
@@ -1161,8 +1161,8 @@
             for j in (0, 2, 1, 3):
                 at = slice(j * UNIT, (j + 1) * UNIT)
                 value = 0.0
-                for p in range(4):
-                    value = value + matmul(branch[:, p * UNIT : (p + 1) * UNIT], w_in[p // 2, p % 2, at, :], NT)
+                for p in range(2):
+                    value = value + matmul(branch[:, 2 * p * UNIT : 2 * (p + 1) * UNIT], w_in[p, at, :], NT)
                 grad[:, at] = value.astype(jnp.bfloat16)
                 if j == 2:
                     far_start(0)
@@ -1224,7 +1224,7 @@
         pltpu.VMEM(tokens.shape, jnp.bfloat16), pltpu.VMEM((tokens.shape[1], block), jnp.bfloat16),
         pltpu.VMEM(tokens.shape, jnp.bfloat16), pltpu.VMEM(tokens.shape, jnp.float32), pltpu.VMEM(tokens.shape, jnp.float32),
         pltpu.VMEM((w_gate.shape[1], block), jnp.bfloat16), pltpu.VMEM(tokens.shape, jnp.bfloat16),
-        pltpu.VMEM(tokens.shape, jnp.float32), pltpu.VMEM((2, 2, tokens.shape[1], UNIT), jnp.bfloat16),
+        pltpu.VMEM(tokens.shape, jnp.float32), pltpu.VMEM((2, tokens.shape[1], 2 * UNIT), jnp.bfloat16),
         pltpu.VMEM((2, UNIT, tokens.shape[1]), jnp.bfloat16),
     )
 

time: 238 us -> 234 us (0.983)
  Pallas kernels: 236 us -> 233 us
    pallas_call x1, Pallas kernels: 178 us -> 175 us  [go_back(): pl.pallas_call(back_kernel, out_shape=(struct((block, width), low), struc...]
where the time goes in v3:
time: 234 us
  Pallas kernels  233 us (100%)
    pallas_call x1, Pallas kernels, go_back(): pl.pallas_call(back_kernel, out_shape=(struct((block, width), low), struc...  175 us
    pallas_call x1, Pallas kernels, go_forward(): pl.pallas_call(front_kernel, out_shape=(struct((block, width), low), stru...  51.7 us
    pallas_call x1, Pallas kernels, deliver(): pl.pallas_call(deliver_kernel, out_shape=tuple((struct(a.shape, a.dtype)...  5.91 us

profile of v3, /device:TPU:0, one launch (start us, length us, event | category | flops | bytes accessed | tf_op | source)
XLA Modules:
  0.0 234.2 jit_solution(3194416848610602605)
XLA Ops:
  0.6 51.7 %go_forward.1 = (bf16[512,1024]{1,0:T(8,128)(2,1)}, bf16[2,4,512,128]{3,2,1,0:T(8,128)(2,1)}, bf16[2,4,512,128]{3,2,1,0:T(8,128)(2,1)}, bf16[2,4,512,128]{3,2,1,...) custom-call(s32[1,2]{1,0:T(1,128)} %limit_ref.3, ...), custom_call_target="tpu_custom_call" | custom-call | tf_op jit(solution)/shard_map/go_forward/pallas_call | solution.py:741
  52.4 175.2 %go_back.1 = (bf16[512,1024]{1,0:T(8,128)(2,1)}, bf16[512,1024]{1,0:T(8,128)(2,1)}, f32[32,2816]{1,0:T(8,128)}, f32[32,2816]{1,0:T(8,128)}, f32[32,1024]{1,0:T(8...) custom-call(s32[1,2]{1,0:T(1,128)} %limit_ref.3, ...), custom_call_target="tpu_custom_call" | custom-call | tf_op jit(solution)/shard_map/go_back/pallas_call | solution.py:1582
  227.6 0.0 copy-start
  227.6 5.9 %deliver.1 = (bf16[512,1024]{1,0:T(8,128)(2,1)}, bf16[512,1024]{1,0:T(8,128)(2,1)}, f32[32,2816]{1,0:T(8,128)}, f32[32,2816]{1,0:T(8,128)}, f32[32,1024]{1,0:T(8...) custom-call(bf16[512,1024]{1,0:T(8,128)(2,1)} %get-tuple-element.56., ...), custom_call_target="tpu_custom_call" | custom-call | tf_op jit(solution)/shard_map/deliver/pallas_call | solution.py:1646
  233.5 0.0 copy-done
  233.6 0.1 reshape.41
  233.7 0.5 dynamic-slice_bitcast_fusion
  (1 shorter events, 0.0 us)
Async XLA Ops:
  227.6 5.9 %copy-start = (f32[2,1,1024]{2,1,0:T(1,128)S(1)}, f32[2,1,1024]{2,1,0:T(1,128)}, u32[]{:S(2)}) copy-start(f32[2,1,1024]{2,1,0:T(1,128)} %get-tuple-element.69) | copy-start | bytes 24580
